TPU v7x, 32 devices: a whole 2x2x4 slice. The times are simulated.
32 devices in a mesh: tok: 4 (over z), hid: 8 (over y, x, core).
Axes of the slice: x: 2, y: 2, z: 4, core: 2. Of those that a mesh axis runs over, the one named last changes fastest.
Arguments:
- tokens: bfloat16 [2048, 1024], P('tok', 'hid'), may hold values from -6 to 6
- cotangent: bfloat16 [2048, 1024], P('tok', 'hid'), may hold values from -6 to 6
- frozen_in: bfloat16 [1024, 16384], P('tok', 'hid'), may hold values from -0.1875 to 0.1875
- frozen_out: bfloat16 [16384, 1024], P('hid', 'tok'), may hold values from -0.046875 to 0.046875
- input_adapter_first: bfloat16 [1024, 128], P('hid'), may hold values from -0.1875 to 0.1875
- input_adapter_second: bfloat16 [128, 16384], P(None, 'hid'), may hold values from -0.5 to 0.5
- adapter_out_a: bfloat16 [16384, 128], P('hid'), may hold values from -0.046875 to 0.046875
- adapter_out_b: bfloat16 [128, 1024], replicated, may hold values from -0.5 to 0.5
Outputs:
- input_gradient: float32 [2048, 1024], P('tok', 'hid')
- grad_in_a: float32 [1024, 128], P('hid')
- grad_in_b: float32 [128, 16384], P(None, 'hid')
- grad_out_a: float32 [16384, 128], P('hid')
- grad_out_b: float32 [128, 1024], P(None, 'hid')
All inputs are finite; a program needn't handle non-finite values.
Results may differ from a plain program's by a relative error of at most 0.0029.
Values may be sent and summed in bfloat16 or wider, within the bound.
A program may use at most 64 MiB of HBM per device.

v0:
```python
import functools
import math

import jax
import jax.numpy as jnp
from jax import lax
from jax.experimental import pallas as pl
from jax.experimental.pallas import tpu as pltpu
from jax.sharding import PartitionSpec as P

ADAPTER_SCALE = 0.5
GELU_K = 0.7978845608
GELU_C = 0.044715
F32 = jnp.float32
BF16 = jnp.bfloat16


def gelu_pair(pre_activation):
    tangent = jnp.tanh(
        GELU_K * (pre_activation + GELU_C * pre_activation * pre_activation * pre_activation)
    )
    value_out = 0.5 * pre_activation * (1.0 + tangent)
    slopes = 0.5 * (1.0 + tangent) + 0.5 * pre_activation * (1.0 - tangent * tangent) * GELU_K * (
        1.0 + 3.0 * GELU_C * pre_activation * pre_activation
    )
    return (value_out, slopes)


def halves(value):
    high = lax.reduce_precision(value, exponent_bits=8, mantissa_bits=7)
    return jnp.concatenate([high.astype(BF16), (value - high).astype(BF16)], axis=1)


def dot(left, right, dims):
    return lax.dot_general(left, right, (dims, ((), ())), preferred_element_type=F32)


def gather_kernel(
    n_tok, n_hid, tokens, cotangent, w_in, w_out, in_a,
    x, c, full_in, full_out, full_a,
    tok_sem, chip_sem, core_sem, first_sem, first_core_sem, own_sem,
):
    t, h = lax.axis_index("tok"), lax.axis_index("hid")
    n_chip = n_hid // 2
    chip, core = h // 2, h % 2
    rows, cols = tokens.shape
    depth = w_in.shape[0]
    width = full_in.shape[1]

    def remote(source, target, sems, where):
        copy = pltpu.make_async_remote_copy(
            src_ref=source, dst_ref=target, send_sem=sems[0], recv_sem=sems[1],
            device_id=where, device_id_type=pl.DeviceIdType.MESH,
        )
        copy.start()
        return copy

    def pair(sems, *where):
        return sems.at[(0,) + where], sems.at[(1,) + where]

    sibling = (t, 2 * chip + 1 - core)
    chips = [(t, 2 * ((chip + e) % n_chip) + core) for e in range(n_chip)]
    toks = [((t + d) % n_tok, h) for d in range(n_tok)]
    barrier = pltpu.get_barrier_semaphore()
    for where in [sibling] + chips[1:] + toks[1:]:
        pl.semaphore_signal(barrier, inc=1, device_id=where, device_id_type=pl.DeviceIdType.MESH)
    pl.semaphore_wait(barrier, n_chip + n_tok - 1)

    def part(array, d, e):
        at_row = pl.multiple_of(((t + n_tok - d) % n_tok) * rows, rows)
        at_col = pl.multiple_of((2 * ((chip + n_chip - e) % n_chip) + core) * cols, cols)
        return array.at[pl.ds(at_row, rows), pl.ds(at_col, cols)]

    def first_part(e):
        at = pl.multiple_of((2 * ((chip + n_chip - e) % n_chip) + core) * cols, cols)
        return full_a.at[pl.ds(at, cols), :]

    both = ((tokens, x), (cotangent, c))
    sent, from_tok, from_chip, from_core, weights = [], [], [], [], []
    for d in range(1, n_tok):
        from_tok.append([
            remote(own, part(whole, 0, 0), pair(tok_sem, d - 1, k), toks[d])
            for k, (own, whole) in enumerate(both)
        ])

    def to_chips(d, blocks):
        from_chip.append([
            [
                remote(blocks[k], part(both[k][1], d, 0), pair(chip_sem, d, e - 1, k), chips[e])
                for k in range(2)
            ]
            for e in range(1, n_chip)
        ])

    def to_core(d, e, blocks):
        for k in range(2):
            from_core.append(
                remote(blocks[k], part(both[k][1], d, e), pair(core_sem, d, e, k), sibling)
            )

    to_chips(0, (tokens, cotangent))
    firsts = [
        remote(in_a, first_part(0), pair(first_sem, e - 1), chips[e]) for e in range(1, n_chip)
    ]
    to_core(0, 0, (tokens, cotangent))
    from_core.append(remote(in_a, first_part(0), pair(first_core_sem, 0), sibling))
    for d in range(1, n_tok):
        at = pl.multiple_of(((t + d) % n_tok) * width, width)
        depths = pl.ds(pl.multiple_of(t * depth, depth), depth)
        weights.append(remote(
            w_in.at[:, pl.ds(at, width)], full_in.at[depths, :], pair(tok_sem, d - 1, 2), toks[d]
        ))
        weights.append(remote(
            w_out.at[pl.ds(at, width), :], full_out.at[:, depths], pair(tok_sem, d - 1, 3), toks[d]
        ))
    at = pl.multiple_of(t * width, width)
    depths = pl.ds(pl.multiple_of(t * depth, depth), depth)
    own = [
        (tokens, part(x, 0, 0)),
        (cotangent, part(c, 0, 0)),
        (w_in.at[:, pl.ds(at, width)], full_in.at[depths, :]),
        (w_out.at[pl.ds(at, width), :], full_out.at[:, depths]),
        (in_a, first_part(0)),
    ]
    own = [
        pltpu.make_async_copy(source, target, own_sem.at[k])
        for k, (source, target) in enumerate(own)
    ]
    for copy in own:
        copy.start()

    def pass_on(d):
        for e in range(1, n_chip):
            for copy in from_chip[d][e - 1]:
                copy.wait_recv()
            to_core(d, e, (part(x, d, e), part(c, d, e)))

    for d in range(1, n_tok):
        for copy in from_tok[d - 1]:
            copy.wait_recv()
        blocks = (part(x, d, 0), part(c, d, 0))
        to_chips(d, blocks)
        to_core(d, 0, blocks)
        pass_on(d - 1)
    for e in range(1, n_chip):
        firsts[e - 1].wait_recv()
        from_core.append(remote(first_part(e), first_part(e), pair(first_core_sem, e), sibling))
    pass_on(n_tok - 1)
    for copy in from_core + weights:
        copy.wait_recv()
    for copy in own:
        copy.wait()
    for group in from_tok + [firsts, from_core, weights]:
        for copy in group:
            copy.wait_send()
    for groups in from_chip:
        for group in groups:
            for copy in group:
                copy.wait_send()


def gather_inputs(tokens, cotangent, frozen_in, frozen_out, in_a):
    n_tok, n_hid = lax.axis_size("tok"), lax.axis_size("hid")
    n_chip = n_hid // 2
    count, features = tokens.shape[0] * n_tok, tokens.shape[1] * n_hid
    width = frozen_in.shape[1] // n_tok
    sems = pltpu.SemaphoreType.DMA
    vmem = pl.BlockSpec(memory_space=pltpu.VMEM)
    whole = pl.BlockSpec(memory_space=pl.ANY)
    return pl.pallas_call(
        functools.partial(gather_kernel, n_tok, n_hid),
        out_shape=(
            jax.ShapeDtypeStruct((count, features), BF16),
            jax.ShapeDtypeStruct((count, features), BF16),
            jax.ShapeDtypeStruct((features, width), BF16),
            jax.ShapeDtypeStruct((width, features), BF16),
            jax.ShapeDtypeStruct((features, in_a.shape[1]), BF16),
        ),
        in_specs=[vmem] * 5,
        out_specs=(whole,) * 5,
        scratch_shapes=[
            sems((2, n_tok - 1, 4)),
            sems((2, n_tok, n_chip - 1, 2)),
            sems((2, n_tok, n_chip, 2)),
            sems((2, n_chip - 1)),
            sems((2, n_chip)),
            sems((5,)),
        ],
        compiler_params=pltpu.CompilerParams(
            collective_id=2, has_side_effects=True, vmem_limit_bytes=56 * 1024 * 1024
        ),
    )(tokens, cotangent, frozen_in, frozen_out, in_a)


def reduce_kernel(
    n_tok, n_hid, dense, terms, oa, ib,
    dx_out, terms_out, oa_out, ib_out,
    core_d, core_t, send_d, send_t, recv_d, recv_t, kept_d, kept_t, tok_send, tok_recv,
    all_t, all_oa, all_ib,
    core_sem, chip_sem, tok_sem, term_sem, grad_sem,
):
    t, h = lax.axis_index("tok"), lax.axis_index("hid")
    n_chip = n_hid // 2
    chip, core = h // 2, h % 2
    rows, cols = dx_out.shape
    count = terms.shape[0]
    width = oa.shape[0]

    def remote(source, target, sems, where):
        return pltpu.make_async_remote_copy(
            src_ref=source, dst_ref=target, send_sem=sems[0], recv_sem=sems[1],
            device_id=where, device_id_type=pl.DeviceIdType.MESH,
        )

    sibling = (t, 2 * chip + 1 - core)
    chips = [(t, 2 * ((chip + e) % n_chip) + core) for e in range(n_chip)]
    toks = [((t + d) % n_tok, h) for d in range(n_tok)]
    barrier = pltpu.get_barrier_semaphore()
    for where in [sibling] + chips[1:] + toks[1:]:
        pl.semaphore_signal(barrier, inc=1, device_id=where, device_id_type=pl.DeviceIdType.MESH)
    pl.semaphore_wait(barrier, n_chip + n_tok - 1)

    def block(index, parity):
        return pl.ds(pl.multiple_of((2 * index + parity) * cols, cols), cols)

    def tok_rows(d):
        return pl.ds(pl.multiple_of(((t + d) % n_tok) * rows, rows), rows)

    chunks = [None] + list(range(1, n_tok)) + [0]
    core_copies, chip_copies, tok_copies = [], [], []
    for q, d in enumerate(chunks):
        group = []
        for e in range(n_chip):
            columns = block((chip + e) % n_chip, 1 - core)
            source = terms.at[:, columns] if d is None else dense.at[tok_rows(d), columns]
            target = core_t.at[e] if d is None else core_d.at[d, e]
            copy = remote(source, target, (core_sem.at[0, q, e], core_sem.at[1, q, e]), sibling)
            copy.start()
            group.append(copy)
        core_copies.append(group)
    for d in range(1, n_tok):
        for k, (source, target) in enumerate(((oa, all_oa), (ib, all_ib))):
            copy = remote(
                source, target.at[t], (grad_sem.at[0, d - 1, k], grad_sem.at[1, d - 1, k]), toks[d]
            )
            copy.start()
            tok_copies.append(copy)

    def over_core(q):
        d, group = chunks[q], []
        for e in range(n_chip):
            core_copies[q][e].wait_recv()
            columns = block((chip + e) % n_chip, core)
            if d is None:
                value = terms[:, columns] + core_t[e]
            else:
                value = dense[tok_rows(d), columns] + core_d[d, e]
            if e == 0:
                if d is None:
                    kept_t[...] = value
                else:
                    kept_d[d] = value
                continue
            sent, got = (send_t, recv_t) if d is None else (send_d.at[d], recv_d.at[d])
            sent[e - 1] = value.astype(BF16)
            copy = remote(
                sent.at[e - 1], got.at[e - 1],
                (chip_sem.at[0, q, e - 1], chip_sem.at[1, q, e - 1]), chips[e],
            )
            copy.start()
            group.append(copy)
        chip_copies.append(group)

    def over_chips(q):
        d = chunks[q]
        for copy in chip_copies[q]:
            copy.wait_recv()
        got = recv_t if d is None else recv_d.at[d]
        value = kept_t[...] if d is None else kept_d[d]
        for e in range(n_chip - 1):
            value = value + got[e].astype(F32)
        if d is None:
            all_t[t] = value.astype(BF16)
            for k in range(1, n_tok):
                copy = remote(
                    all_t.at[t], all_t.at[t], (term_sem.at[0, k - 1], term_sem.at[1, k - 1]), toks[k]
                )
                copy.start()
                tok_copies.append(copy)
        elif d == 0:
            kept_d[0] = value
        else:
            tok_send[d - 1] = value.astype(BF16)
            copy = remote(
                tok_send.at[d - 1], tok_recv.at[d - 1],
                (tok_sem.at[0, d - 1], tok_sem.at[1, d - 1]), toks[d],
            )
            copy.start()
            tok_copies.append(copy)

    over_core(0)
    for q in range(1, n_tok + 1):
        over_core(q)
        over_chips(q - 1)
    all_oa[t] = oa[...]
    all_ib[t] = ib[...]
    over_chips(n_tok)
    for copy in tok_copies:
        copy.wait_recv()
    for k in range(n_tok):
        oa_out[pl.ds(k * width, width), :] = all_oa[k].astype(F32)
        ib_out[:, pl.ds(k * width, width)] = all_ib[k].astype(F32)
    value = all_t[0].astype(F32)
    for k in range(1, n_tok):
        value = value + all_t[k].astype(F32)
    terms_out[...] = value
    value = kept_d[0]
    for d in range(1, n_tok):
        value = value + tok_recv[d - 1].astype(F32)
    dx_out[...] = value
    for group in core_copies + chip_copies + [tok_copies]:
        for copy in group:
            copy.wait_send()


def reduce_outputs(dense, terms, oa, ib):
    n_tok, n_hid = lax.axis_size("tok"), lax.axis_size("hid")
    n_chip = n_hid // 2
    rows, cols = dense.shape[0] // n_tok, dense.shape[1] // n_hid
    count = terms.shape[0]
    width, rank = oa.shape
    sems = pltpu.SemaphoreType.DMA
    vmem = pl.BlockSpec(memory_space=pltpu.VMEM)
    return pl.pallas_call(
        functools.partial(reduce_kernel, n_tok, n_hid),
        out_shape=(
            jax.ShapeDtypeStruct((rows, cols), F32),
            jax.ShapeDtypeStruct((count, cols), F32),
            jax.ShapeDtypeStruct((n_tok * width, rank), F32),
            jax.ShapeDtypeStruct((rank, n_tok * width), F32),
        ),
        in_specs=[vmem] * 4,
        out_specs=(vmem,) * 4,
        scratch_shapes=[
            pltpu.VMEM((n_tok, n_chip, rows, cols), F32),
            pltpu.VMEM((n_chip, count, cols), F32),
            pltpu.VMEM((n_tok, n_chip - 1, rows, cols), BF16),
            pltpu.VMEM((n_chip - 1, count, cols), BF16),
            pltpu.VMEM((n_tok, n_chip - 1, rows, cols), BF16),
            pltpu.VMEM((n_chip - 1, count, cols), BF16),
            pltpu.VMEM((n_tok, rows, cols), F32),
            pltpu.VMEM((count, cols), F32),
            pltpu.VMEM((n_tok - 1, rows, cols), BF16),
            pltpu.VMEM((n_tok - 1, rows, cols), BF16),
            pltpu.VMEM((n_tok, count, cols), BF16),
            pltpu.VMEM((n_tok, width, rank), BF16),
            pltpu.VMEM((n_tok, rank, width), BF16),
            sems((2, n_tok + 1, n_chip)),
            sems((2, n_tok + 1, n_chip - 1)),
            sems((2, n_tok - 1)),
            sems((2, n_tok - 1)),
            sems((2, n_tok - 1, 2)),
        ],
        compiler_params=pltpu.CompilerParams(
            collective_id=1, has_side_effects=True, vmem_limit_bytes=56 * 1024 * 1024
        ),
    )(dense, terms, oa, ib)


def local(tokens, cotangent, frozen_in, frozen_out, in_a, in_b, out_a, out_b):
    n_tok, t = lax.axis_size("tok"), lax.axis_index("tok")
    rank = in_b.shape[0]
    count = tokens.shape[0] * n_tok
    scale = ADAPTER_SCALE / math.sqrt(count)
    width = frozen_in.shape[1] // n_tok
    x, c, w_in, w_out, in_a_full = gather_inputs(tokens, cotangent, frozen_in, frozen_out, in_a)
    second = lax.dynamic_slice_in_dim(in_b, t * width, width, 1)
    first = lax.dynamic_slice_in_dim(out_a, t * width, width, 0)
    half_second = (ADAPTER_SCALE * second).astype(BF16)
    half_first = (ADAPTER_SCALE * first).astype(BF16)
    half_in_a = (ADAPTER_SCALE * in_a_full).astype(BF16)
    low_in = halves(dot(x, in_a_full, ((1,), (0,))))
    back_low = halves(dot(c, out_b, ((1,), (1,))))
    pre = dot(x, w_in, ((1,), (0,))) + dot(
        low_in, jnp.concatenate([half_second, half_second], axis=0), ((1,), (0,))
    )
    value_out, slopes = gelu_pair(pre)
    act = value_out.astype(BF16)
    dense_back = dot(c, w_out, ((1,), (1,))) + dot(
        back_low, jnp.concatenate([half_first, half_first], axis=1), ((1,), (1,))
    )
    grad_pre = (dense_back * slopes).astype(BF16)
    oa = dot(act, back_low, ((0,), (0,)))
    oa = scale * (oa[:, :rank] + oa[:, rank:])
    ib = dot(low_in, grad_pre, ((0,), (0,)))
    ib = scale * (ib[:rank] + ib[rank:])
    rank_out = halves(dot(act, first, ((1,), (0,))))
    rank_back = halves(dot(grad_pre, second, ((1,), (1,))))
    dense = dot(grad_pre, w_in, ((1,), (1,))) + dot(
        rank_back, jnp.concatenate([half_in_a, half_in_a], axis=1), ((1,), (1,))
    )
    out_term = dot(rank_out, c, ((0,), (0,)))
    in_term = dot(rank_back, x, ((0,), (0,)))
    terms = scale * jnp.concatenate(
        [out_term[:rank] + out_term[rank:], in_term[:rank] + in_term[rank:]], axis=0
    )
    input_gradient, total, grad_out_a, grad_in_b = reduce_outputs(
        dense, terms, oa.astype(BF16), ib.astype(BF16)
    )
    return (input_gradient, total[rank:].T, grad_in_b, grad_out_a, total[:rank])


def local_by_rows(
    tokens,
    cotangent,
    frozen_in,
    frozen_out,
    input_adapter_first,
    input_adapter_second,
    adapter_out_a,
    adapter_out_b,
):
    highest_precision = lax.Precision.HIGHEST
    device_local_rows = tokens.shape[0]
    rank_width = input_adapter_second.shape[0]
    gradient_scale = ADAPTER_SCALE / math.sqrt(device_local_rows * lax.axis_size("tok"))
    full_tokens, full_cotan = (
        lax.all_gather(tokens, "hid", axis=1, tiled=True),
        lax.all_gather(cotangent, "hid", axis=1, tiled=True),
    )
    in_rows = lax.all_gather(frozen_in, "tok", axis=0, tiled=True)
    in_a_full = lax.all_gather(input_adapter_first, "hid", axis=0, tiled=True)
    lowrank_input = jnp.dot(full_tokens, in_a_full, preferred_element_type=jnp.float32)
    second_float = input_adapter_second.astype(jnp.float32)
    out_a_float = adapter_out_a.astype(jnp.float32)
    pre_activation = jnp.dot(
        full_tokens, in_rows, preferred_element_type=jnp.float32
    ) + ADAPTER_SCALE * jnp.dot(lowrank_input, second_float, precision=highest_precision)
    value_out, slopes = gelu_pair(pre_activation)
    hidden_act = value_out.astype(jnp.bfloat16)
    backward_lowrank = jnp.einsum(
        "td,rd->tr", full_cotan, adapter_out_b, preferred_element_type=jnp.float32
    )
    rank_out = jnp.dot(hidden_act, adapter_out_a, preferred_element_type=jnp.float32)
    dense_backward = jnp.einsum(
        "td,fd->tf",
        full_cotan,
        lax.all_gather(frozen_out, "tok", axis=1, tiled=True),
        preferred_element_type=jnp.float32,
    )
    dense_backward = dense_backward + ADAPTER_SCALE * jnp.dot(
        backward_lowrank, out_a_float.T, precision=highest_precision
    )
    grad_pre = (dense_backward * slopes).astype(jnp.bfloat16)
    rank_backward = jnp.einsum(
        "tf,rf->tr", grad_pre, input_adapter_second, preferred_element_type=jnp.float32
    )
    dense_in = jnp.einsum("tf,df->td", grad_pre, in_rows, preferred_element_type=jnp.float32)
    grad_out_a = gradient_scale * jnp.dot(
        hidden_act.astype(jnp.float32).T, backward_lowrank, precision=highest_precision
    )
    grad_in_b = gradient_scale * jnp.dot(
        lowrank_input.T, grad_pre.astype(jnp.float32), precision=highest_precision
    )
    in_a_float = in_a_full.astype(jnp.float32)
    dx_term = dense_in + ADAPTER_SCALE * jnp.dot(
        rank_backward, in_a_float.T, precision=highest_precision
    )
    out_term = jnp.dot(rank_out.T, full_cotan.astype(jnp.float32), precision=highest_precision)
    in_term = jnp.dot(rank_backward.T, full_tokens.astype(jnp.float32), precision=highest_precision)
    rank_terms = jnp.concatenate([out_term, in_term], axis=0)
    input_gradient, rank_local = (
        lax.psum_scatter(dx_term, "hid", scatter_dimension=1, tiled=True),
        lax.psum_scatter(rank_terms, "hid", scatter_dimension=1, tiled=True),
    )
    grad_out_a, grad_in_b, rank_total = lax.psum((grad_out_a, grad_in_b, rank_local), "tok")
    grad_out_b = gradient_scale * rank_total[:rank_width]
    grad_in_a = gradient_scale * rank_total[rank_width:].T
    return (input_gradient, grad_in_a, grad_in_b, grad_out_a, grad_out_b)


def solution(mesh):
    in_specs = (
        P("tok", "hid"),
        P("tok", "hid"),
        P("tok", "hid"),
        P("hid", "tok"),
        P("hid", None),
        P(None, "hid"),
        P("hid", None),
        P(),
    )
    out_specs = (P("tok", "hid"), P("hid", None), P(None, "hid"), P("hid", None), P(None, "hid"))
    def body(*arrays):
        share = arrays[2].shape[1] // lax.axis_size("tok")
        return local(*arrays) if share % 128 == 0 else local_by_rows(*arrays)

    return jax.shard_map(body, mesh=mesh, in_specs=in_specs, out_specs=out_specs, check_vma=False)
```

profile of v0, /device:TPU:0, one launch (start us, length us, event | category | flops | bytes accessed | tf_op | source)
XLA Modules:
  0.0 169.2 jit_solution(3461243369972474223)
XLA Ops:
  0.6 0.0 copy-start
  0.7 1.0 dynamic-slice_multiply_fusion
  1.6 0.9 dynamic-slice_multiply_fusion.1
  2.6 67.5 %shard_map.119 = (bf16[2048,1024]{1,0:T(8,128)(2,1)}, bf16[2048,1024]{1,0:T(8,128)(2,1)}, bf16[1024,512]{1,0:T(8,128)(2,1)}, bf16[512,1024]{1,0:T(8,128)(2,1)}, bf16[1024,128]{1,0:T(8,128)(2,1)}) custom-call(bf16[512,128]{1,0:T(8,128)(2,1)} %tokens.1, bf16[512,128]{1,0:T(8,128)(2,1)} %cotangent.1, bf16[256,2048]{1,0:T(8,128)(2,1)} %w_in.1, ...), custom_call_target="tpu_custom_call" | custom-call | tf_op jit(solution)/shard_map/pallas_call | solution.py:170
  70.1 0.0 copy-start.2
  70.1 1.1 broadcast_multiply_fusion
  71.2 3.9 %reduce-precision_convert_fusion.2 = (bf16[2048,128]{0,1:T(8,128)(2,1)S(1)}, bf16[2048,128]{0,1:T(8,128)(2,1)S(1)}) fusion(bf16[2048,1024]{1,0:T(8,128)(2,1)} %get-tuple-element.16, bf16[1024,128]{1,0:T(8,128)(2,1)} %get-tuple-element.18), kind=kOutput, calls=%fused_computation.17 | convolution fusion | flops 537919488 | bytes 5505024 | tf_op jit(solution)/shard_map/dot_general | solution.py:35
  75.2 0.0 copy-start.4
  75.2 0.0 copy-done
  75.2 0.0 copy-done.2
  75.2 1.5 reduce-precision_convert_fusion.3
  76.7 0.0 copy-done.4
  76.8 0.0 copy-start.1
  76.8 0.0 copy-start.3
  76.8 2.4 %fusion.45 = f32[2048,512]{1,0:T(8,128)S(1)} fusion(bf16[2048,1024]{1,0:T(8,128)(2,1)S(1)} %copy-done.2, bf16[512,1024]{1,0:T(8,128)(2,1)S(1)} %copy-done.4), kind=kOutput, calls=%fused_computation.70 | convolution fusion | flops 2147483648 | bytes 9437184 | tf_op jit(solution)/shard_map/dot_general | solution.py:35
  79.2 0.0 copy-done.1
  79.2 0.0 copy-done.3
  79.2 2.4 %fusion.46 = f32[2048,512]{1,0:T(8,128)S(1)} fusion(bf16[2048,1024]{1,0:T(8,128)(2,1)S(1)} %copy-done.1, bf16[1024,512]{1,0:T(8,128)(2,1)S(1)} %copy-done.3), kind=kOutput, calls=%fused_computation.71 | convolution fusion | flops 2147483648 | bytes 9437184 | tf_op jit(solution)/shard_map/dot_general | solution.py:35
  81.6 0.8 convolution_add_fusion.1
  82.4 3.4 %fusion.6 = bf16[2048,512]{1,0:T(8,128)(2,1)S(1)} fusion(f32[2048,512]{1,0:T(8,128)S(1)} %convolution_add_fusion.1, f32[2048,512]{1,0:T(8,128)S(1)} %fusion.45, bf16[2048,128]{0,1:T(8,128)(2,1)S(1)} %get-tuple-element.33, bf16[2048,128]{0,1:T(8,128)(2,1)S(1)} %get-tuple-element.32, bf16[512,128]{1,0:T(8,128)(2,1)S(1)} %dynamic-slice_multiply_fusion.1), kind=kOutput, calls=%fused_computation.9 | convolution fusion | flops 560463872 | bytes 11665408 | tf_op jit(solution)/shard_map/dot_general | solution.py:35
  85.8 1.5 fusion.17
  87.4 2.6 %reduce-precision_convert_fusion = (bf16[2048,128]{0,1:T(8,128)(2,1)S(1)}, bf16[2048,128]{0,1:T(8,128)(2,1)S(1)}) fusion(bf16[2048,128]{1,0:T(8,128)(2,1)} %param.14, s32[]{:T(128)S(6)} %select_n.4, f32[2048,512]{1,0:T(8,128)S(1)} %convolution_add_fusion.1), kind=kOutput, calls=%fused_computation.13 | convolution fusion | flops 278921216 | bytes 5373956 | tf_op jit(solution)/shard_map/dot_general | solution.py:35
  89.9 0.7 fusion.16
  90.6 0.7 fusion.22.ib
  91.3 0.7 fusion.24.oa
  92.0 1.3 fusion.11
  93.3 1.7 %reduce-precision_convert_fusion.1 = (bf16[2048,128]{0,1:T(8,128)(2,1)S(1)}, bf16[2048,128]{0,1:T(8,128)(2,1)S(1)}) fusion(bf16[2048,512]{1,0:T(8,128)(2,1)S(1)} %fusion.6, bf16[128,2048]{1,0:T(8,128)(2,1)} %param.13, s32[]{:T(128)S(6)} %select_n.4), kind=kOutput, calls=%fused_computation.15 | convolution fusion | flops 269484032 | bytes 3276804 | tf_op jit(solution)/shard_map/dot_general | solution.py:35
  95.1 1.3 fusion.15
  96.3 0.2 slice_add_fusion
  96.5 1.1 maximum_multiply_fusion.terms
  97.6 2.4 %fusion.47 = f32[2048,1024]{1,0:T(8,128)S(1)} fusion(bf16[2048,512]{1,0:T(8,128)(2,1)S(1)} %fusion.6, bf16[1024,512]{1,0:T(8,128)(2,1)S(1)} %copy-done.3), kind=kOutput, calls=%fused_computation.72 | convolution fusion | flops 2147483648 | bytes 11534336 | tf_op jit(solution)/shard_map/dot_general | solution.py:35
  100.0 4.5 %convolution_add_fusion.dense = f32[2048,1024]{1,0:T(8,128)} fusion(f32[2048,1024]{1,0:T(8,128)S(1)} %fusion.47, bf16[2048,128]{0,1:T(8,128)(2,1)S(1)} %get-tuple-element.31, bf16[2048,128]{0,1:T(8,128)(2,1)S(1)} %get-tuple-element.30, bf16[1024,128]{1,0:T(8,128)(2,1)S(1)} %broadcast_multiply_fusion), kind=kOutput, calls=%fused_computation.2 | convolution fusion | flops 1078984704 | bytes 18087936 | tf_op jit(solution)/shard_map/dot_general | solution.py:35
  104.5 56.2 %shard_map.120 = (f32[512,128]{1,0:T(8,128)}, f32[256,128]{1,0:T(8,128)}, f32[2048,128]{1,0:T(8,128)}, f32[128,2048]{1,0:T(8,128)}) custom-call(f32[2048,1024]{1,0:T(8,128)} %convolution_add_fusion.dense, f32[256,1024]{1,0:T(8,128)} %maximum_multiply_fusion.terms, bf16[512,128]{1,0:T(8,128)(2,1)} %fusion.24.oa, bf16[128,512]{1,0:T(8,128)(2,1)} %fusion.22.ib), custom_call_target="tpu_custom_call" | custom-call | tf_op jit(solution)/shard_map/pallas_call | solution.py:334
  160.7 1.5 fusion.44
  162.2 0.7 copy.13
  162.9 1.7 copy.17
  164.6 2.3 %copy.18 = f32[128,2048]{1,0:T(8,128)} copy(f32[128,2048]{1,0:T(8,128)} %get-tuple-element.47) | data formatting | bytes 2097152
  166.9 2.3 %copy.19 = f32[2048,128]{1,0:T(8,128)} copy(f32[2048,128]{1,0:T(8,128)} %get-tuple-element.48) | data formatting | bytes 2097152
Async XLA Ops:
  0.6 74.6 %copy-start = (bf16[128,1024]{1,0:T(8,128)(2,1)S(1)}, bf16[128,1024]{1,0:T(8,128)(2,1)}, u32[]{:S(2)}) copy-start(bf16[128,1024]{1,0:T(8,128)(2,1)} %param.15) | copy-start | bytes 786436
  70.1 5.1 %copy-start.2 = (bf16[2048,1024]{1,0:T(8,128)(2,1)S(1)}, bf16[2048,1024]{1,0:T(8,128)(2,1)}, u32[]{:S(2)}) copy-start(bf16[2048,1024]{1,0:T(8,128)(2,1)} %get-tuple-element.14) | copy-start | bytes 12582916
  75.2 1.6 copy-start.4
  76.8 2.5 %copy-start.1 = (bf16[2048,1024]{1,0:T(8,128)(2,1)S(1)}, bf16[2048,1024]{1,0:T(8,128)(2,1)}, u32[]{:S(2)}) copy-start(bf16[2048,1024]{1,0:T(8,128)(2,1)} %get-tuple-element.16) | copy-start | bytes 12582916
  76.8 2.5 %copy-start.3 = (bf16[1024,512]{1,0:T(8,128)(2,1)S(1)}, bf16[1024,512]{1,0:T(8,128)(2,1)}, u32[]{:S(2)}) copy-start(bf16[1024,512]{1,0:T(8,128)(2,1)} %get-tuple-element.17) | copy-start | bytes 3145732
where the time goes:
time: 170 us; the launch traced here: 169 us
  Pallas kernels  124 us (73%)
  matrix products  30.4 us (18%)
  local copies, waits for them, and re-layouts  8.51 us (5%)
  other arithmetic  5.68 us (3%)
    pallas_call x1, Pallas kernels, gather_inputs(): pl.pallas_call(functools.partial(gather_kernel, n_tok, n_hid), out_shape=...  67.5 us
    pallas_call x1, Pallas kernels, reduce_outputs(): pl.pallas_call(functools.partial(reduce_kernel, n_tok, n_hid), out_shape=...  56.2 us
    dot_general x14, matrix products, dot(): lax.dot_general(left, right, (dims, ((), ())), preferred_element_type=F32)  30.4 us
    unnamed x14, local copies, waits for them, and re-layouts  7 us

commit v1 on v0

v1 whole, which is shorter than its diff:
```python
import functools
import math

import jax
import jax.numpy as jnp
from jax import lax
from jax.experimental import pallas as pl
from jax.experimental.pallas import tpu as pltpu
from jax.sharding import PartitionSpec as P

ADAPTER_SCALE = 0.5
GELU_K = 0.7978845608
GELU_C = 0.044715
F32 = jnp.float32
BF16 = jnp.bfloat16


def gelu_pair(pre_activation):
    tangent = jnp.tanh(
        GELU_K * (pre_activation + GELU_C * pre_activation * pre_activation * pre_activation)
    )
    value_out = 0.5 * pre_activation * (1.0 + tangent)
    slopes = 0.5 * (1.0 + tangent) + 0.5 * pre_activation * (1.0 - tangent * tangent) * GELU_K * (
        1.0 + 3.0 * GELU_C * pre_activation * pre_activation
    )
    return (value_out, slopes)


def dot(left, right, dims):
    return lax.dot_general(left, right, (dims, ((), ())), preferred_element_type=F32)


def nn(left, right):
    return dot(left, right, ((1,), (0,)))


def nt(left, right):
    return dot(left, right, ((1,), (1,)))


def tn(left, right):
    return dot(left, right, ((0,), (0,)))


def split(value):
    high = value.astype(BF16)
    return high, (value - high.astype(F32)).astype(BF16)


def fused_kernel(
    n_tok, n_hid, n_part, scale,
    tokens, cotangent, w_in, w_out, in_a, in_b, out_a, out_b,
    dx_out, terms_out, oa_all, ib_all,
    x, c, full_in, full_out, full_a, b_mat, second, first, second2, first2, a2,
    low, back, pre_s, back_s, act_s, grad_s, dense, rank_out, rank_back, oa_acc, ib_acc, terms,
    core_d, core_t, send_d, send_t, recv_d, recv_t, kept_d, kept_t, tok_send, tok_recv, all_t,
    act_send, act_recv, chip_sem, core_sem, first_sem, first_core_sem, w_sem, own_sem,
    core_r_sem, chip_r_sem, tok_sem, term_sem, grad_send, grad_recv,
):
    t, h = lax.axis_index("tok"), lax.axis_index("hid")
    n_chip = n_hid // 2
    chip, core = h // 2, h % 2
    rows, cols = tokens.shape
    depth = w_in.shape[0]
    width = full_in.shape[1]
    part_width = width // n_part
    rank = full_a.shape[1]

    def remote(source, target, send, recv, where):
        return pltpu.make_async_remote_copy(
            src_ref=source, dst_ref=target, send_sem=send, recv_sem=recv,
            device_id=where, device_id_type=pl.DeviceIdType.MESH,
        )

    def begin(*arguments):
        copy = remote(*arguments)
        copy.start()
        return copy

    sibling = (t, 2 * chip + 1 - core)
    chips = [(t, 2 * ((chip + e) % n_chip) + core) for e in range(n_chip)]
    toks = [((t + d) % n_tok, h) for d in range(n_tok)]
    barrier = pltpu.get_barrier_semaphore()
    for where in [sibling] + chips[1:] + toks[1:]:
        pl.semaphore_signal(barrier, inc=1, device_id=where, device_id_type=pl.DeviceIdType.MESH)
    pl.semaphore_wait(barrier, n_chip + n_tok - 1)

    orders = [sorted(range(n_tok), key=lambda s: (abs(s - k), s)) for k in range(n_tok)]
    sources = [t]
    for j in range(1, n_tok):
        source = jnp.int32(orders[0][j])
        for k in range(1, n_tok):
            source = jnp.where(t == k, jnp.int32(orders[k][j]), source)
        sources.append(source)

    def row_at(source):
        return pl.multiple_of(source * rows, rows)

    def part(array, source, e):
        at_col = pl.multiple_of((2 * ((chip + n_chip - e) % n_chip) + core) * cols, cols)
        return array.at[pl.ds(row_at(source), rows), pl.ds(at_col, cols)]

    def along(source, blocks, send, recv, act):
        @pl.when((source <= t) & (t + 1 < n_tok))
        def _():
            for k, (block, target) in enumerate(blocks):
                act(remote(block, target, send(0, source, k), recv(source, k), (t + 1, h)))

        @pl.when((source >= t) & (t > 0))
        def _():
            for k, (block, target) in enumerate(blocks):
                act(remote(block, target, send(1, source, k), recv(source, k), (t - 1, h)))

    def start(copy):
        copy.start()

    def wait_send(copy):
        copy.wait_send()

    def act_blocks(j):
        source = sources[j]
        mine = (tokens, cotangent)
        return [
            (mine[k] if j == 0 else part(array, source, 0), part(array, source, 0))
            for k, array in enumerate((x, c))
        ]

    def act_along(j, act):
        along(
            sources[j], act_blocks(j),
            lambda way, source, k: act_send.at[way, source, k],
            lambda source, k: act_recv.at[source, k], act,
        )

    from_chip, from_core = {}, {}

    def to_chips(j):
        for e in range(1, n_chip):
            from_chip[j, e] = [
                begin(block, target, chip_sem.at[0, j, e - 1, k], chip_sem.at[1, j, e - 1, k], chips[e])
                for k, (block, target) in enumerate(act_blocks(j))
            ]

    def to_core(j, e):
        if e == 0:
            blocks = act_blocks(j)
        else:
            blocks = [(part(array, sources[j], e),) * 2 for array in (x, c)]
        from_core[j, e] = [
            begin(block, target, core_sem.at[0, j, e, k], core_sem.at[1, j, e, k], sibling)
            for k, (block, target) in enumerate(blocks)
        ]

    def first_part(e):
        at = pl.multiple_of((2 * ((chip + n_chip - e) % n_chip) + core) * cols, cols)
        return full_a.at[pl.ds(at, cols), :]

    weights = {}
    depths = pl.ds(pl.multiple_of(t * depth, depth), depth)

    def weight_blocks(d, p):
        at = pl.multiple_of(((t + d) % n_tok) * width + p * part_width, part_width)
        here = pl.ds(p * part_width, part_width)
        return [
            (w_in.at[:, pl.ds(at, part_width)], full_in.at[depths, here]),
            (w_out.at[pl.ds(at, part_width), :], full_out.at[here, depths]),
        ]

    def send_weight(d, p, k):
        block, target = weight_blocks(d, p)[k]
        weights[d, p, k] = begin(
            block, target, w_sem.at[0, d - 1, p, k], w_sem.at[1, d - 1, p, k], toks[d]
        )

    act_along(0, start)
    to_chips(0)
    firsts = [
        begin(in_a, first_part(0), first_sem.at[0, e - 1], first_sem.at[1, e - 1], chips[e])
        for e in range(1, n_chip)
    ]
    to_core(0, 0)
    a_core = [begin(in_a, first_part(0), first_core_sem.at[0, 0], first_core_sem.at[1, 0], sibling)]
    for d in range(1, n_tok):
        send_weight(d, 0, 0)
    at = pl.multiple_of(t * width, width)
    own = [(block, target) for block, target in act_blocks(0)]
    own += [(in_a, first_part(0)), (out_b, b_mat)]
    own += [(in_b.at[:, pl.ds(at, width)], second), (out_a.at[pl.ds(at, width), :], first)]
    for p in range(n_part):
        own += weight_blocks(0, p)
    own = [
        pltpu.make_async_copy(block, target, own_sem.at[k])
        for k, (block, target) in enumerate(own)
    ]
    for copy in own:
        copy.start()

    def arrive(j):
        for k, (block, target) in enumerate(act_blocks(j)):
            remote(
                target, target, act_send.at[0, sources[j], k], act_recv.at[sources[j], k], sibling
            ).wait_recv()
        act_along(j, start)
        to_chips(j)
        to_core(j, 0)

    def pass_on(j):
        for e in range(1, n_chip):
            for copy in from_chip[j, e]:
                copy.wait_recv()
            to_core(j, e)

    def complete(j):
        for e in range(n_chip):
            for copy in from_core[j, e]:
                copy.wait_recv()

    def ranks(source):
        here = pl.ds(row_at(source), rows)
        high, rest = split(nn(x[here, :], full_a[...]))
        low[here, :rank] = high
        low[here, rank:] = rest
        high, rest = split(nt(c[here, :], b_mat[...]))
        back[here, :rank] = high
        back[here, rank:] = rest

    def hidden(p, source, begun):
        here = pl.ds(row_at(source), rows)
        those = slice(p * part_width, (p + 1) * part_width)
        pre_s[...] = nn(x[here, :], full_in[:, those]) + nn(low[here, :], second2[:, those])
        back_s[...] = nt(c[here, :], full_out[those, :]) + nt(back[here, :], first2[those, :])
        step = rows // 8
        for at in range(0, rows, step):
            some = slice(at, at + step)
            value_out, slopes = gelu_pair(pre_s[some, :])
            act_s[some, :] = value_out.astype(BF16)
            grad_s[some, :] = (back_s[some, :] * slopes).astype(BF16)
        act, grad = act_s[...], grad_s[...]
        oa_new, ib_new = tn(act, back[here, :]), tn(low[here, :], grad)
        out_new, back_new = nn(act, first[those, :]), nt(grad, second[:, those])
        if begun:
            oa_acc[p] += oa_new
            ib_acc[p] += ib_new
        else:
            oa_acc[p] = oa_new
            ib_acc[p] = ib_new
        if p == 0:
            rank_out[here, :] = out_new
            rank_back[here, :] = back_new
        else:
            rank_out[here, :] += out_new
            rank_back[here, :] += back_new
        if p < n_part - 1:
            if p == 0:
                dense[here, :] = nt(grad, full_in[:, those])
            else:
                dense[here, :] += nt(grad, full_in[:, those])
            return
        high, rest = split(rank_back[here, :])
        low[here, :rank] = high
        low[here, rank:] = rest
        high, rest = split(rank_out[here, :])
        back[here, :rank] = high
        back[here, rank:] = rest
        value = nt(grad, full_in[:, those]) + nt(low[here, :], a2[...])
        dense[here, :] = dense[here, :] + value if n_part > 1 else value

    for j in range(1, n_tok):
        arrive(j)
        if j == 1:
            for d in range(1, n_tok):
                send_weight(d, 0, 1)
            for e in range(1, n_chip):
                firsts[e - 1].wait_recv()
                a_core.append(begin(
                    first_part(e), first_part(e), first_core_sem.at[0, e], first_core_sem.at[1, e],
                    sibling,
                ))
        if j == n_tok - 1:
            for p in range(1, n_part):
                for d in range(1, n_tok):
                    for k in range(2):
                        send_weight(d, p, k)
        pass_on(j - 1)
        if j == 1:
            for copy in own:
                copy.wait()
            for copy in a_core:
                copy.wait_recv()
            half = (ADAPTER_SCALE * second[...].astype(F32)).astype(BF16)
            second2[:rank, :] = half
            second2[rank:, :] = half
            half = (ADAPTER_SCALE * first[...].astype(F32)).astype(BF16)
            first2[:, :rank] = half
            first2[:, rank:] = half
            half = (ADAPTER_SCALE * full_a[...].astype(F32)).astype(BF16)
            a2[:, :rank] = half
            a2[:, rank:] = half
        complete(j - 1)
        ranks(sources[j - 1])

    def wait_weights(p):
        for d in range(1, n_tok):
            for k in range(2):
                weights[d, p, k].wait_recv()

    def oa_blocks(source, p):
        at = pl.multiple_of(source * width + p * part_width, part_width)
        oa_at, ib_at = oa_all.at[pl.ds(at, part_width), :], ib_all.at[:, pl.ds(at, part_width)]
        return [(oa_at, oa_at), (ib_at, ib_at)]

    def oa_along(j, p, act):
        along(
            sources[j], oa_blocks(sources[j], p),
            lambda way, source, k: grad_send.at[way, source, p, k],
            lambda source, k: grad_recv.at[source, p, k], act,
        )

    def finish_grads(p):
        at = pl.multiple_of(t * width + p * part_width, part_width)
        oa = oa_acc[p]
        oa_all[pl.ds(at, part_width), :] = (scale * (oa[:, :rank] + oa[:, rank:])).astype(BF16)
        ib = ib_acc[p]
        ib_all[:, pl.ds(at, part_width)] = (scale * (ib[:rank] + ib[rank:])).astype(BF16)
        oa_along(0, p, start)

    def relay_grads(j, p):
        for k, (block, target) in enumerate(oa_blocks(sources[j], p)):
            remote(
                target, target, grad_send.at[0, sources[j], p, k], grad_recv.at[sources[j], p, k],
                sibling,
            ).wait_recv()
        oa_along(j, p, start)

    wait_weights(0)
    if n_part > 1:
        for j in range(n_tok - 1):
            hidden(0, sources[j], j > 0)
    pass_on(n_tok - 1)
    complete(n_tok - 1)
    ranks(sources[n_tok - 1])
    if n_part > 1:
        hidden(0, sources[n_tok - 1], True)
        finish_grads(0)
    for p in range(1, n_part - 1):
        wait_weights(p)
        for j in range(n_tok):
            hidden(p, sources[j], j > 0)
        finish_grads(p)
    last = n_part - 1
    if last > 0:
        wait_weights(last)

    def block(index, parity):
        return pl.ds(pl.multiple_of((2 * index + parity) * cols, cols), cols)

    def tok_rows(d):
        return pl.ds(row_at((t + d) % n_tok), rows)

    chunks = list(range(1, n_tok)) + [0, None]
    core_copies, chip_copies, tok_copies = {}, {}, []

    def to_sibling(q):
        d = chunks[q]
        core_copies[q] = []
        for e in range(n_chip):
            columns = block((chip + e) % n_chip, 1 - core)
            source = terms.at[:, columns] if d is None else dense.at[tok_rows(d), columns]
            target = core_t.at[e] if d is None else core_d.at[d, e]
            core_copies[q].append(
                begin(source, target, core_r_sem.at[0, q, e], core_r_sem.at[1, q, e], sibling)
            )

    def over_core(q):
        d = chunks[q]
        chip_copies[q] = []
        for e in list(range(1, n_chip)) + [0]:
            core_copies[q][e].wait_recv()
            columns = block((chip + e) % n_chip, core)
            if d is None:
                value = terms[:, columns] + core_t[e]
            else:
                value = dense[tok_rows(d), columns] + core_d[d, e]
            if e == 0:
                if d is None:
                    kept_t[...] = value
                else:
                    kept_d[d] = value
                continue
            sent, got = (send_t, recv_t) if d is None else (send_d.at[d], recv_d.at[d])
            sent[e - 1] = value.astype(BF16)
            chip_copies[q].append(begin(
                sent.at[e - 1], got.at[e - 1],
                chip_r_sem.at[0, q, e - 1], chip_r_sem.at[1, q, e - 1], chips[e],
            ))

    def over_chips(q):
        d = chunks[q]
        for copy in chip_copies[q]:
            copy.wait_recv()
        got = recv_t if d is None else recv_d.at[d]
        value = kept_t[...] if d is None else kept_d[d]
        for e in range(n_chip - 1):
            value = value + got[e].astype(F32)
        if d is None:
            all_t[t] = value.astype(BF16)
            for k in range(1, n_tok):
                tok_copies.append(begin(
                    all_t.at[t], all_t.at[t], term_sem.at[0, k - 1], term_sem.at[1, k - 1], toks[k]
                ))
        elif d == 0:
            kept_d[0] = value
        else:
            tok_send[d - 1] = value.astype(BF16)
            tok_copies.append(begin(
                tok_send.at[d - 1], tok_recv.at[d - 1],
                tok_sem.at[0, d - 1], tok_sem.at[1, d - 1], toks[d],
            ))

    for q in range(n_tok):
        hidden(last, (t + chunks[q]) % n_tok, q > 0)
        to_sibling(q)
        if q >= 1:
            over_core(q - 1)
        if q >= 2:
            over_chips(q - 2)
            for p in range(last):
                relay_grads(q - 1, p)
    finish_grads(last)
    over_core(n_tok - 1)
    out_cols = x.shape[1] // n_chip
    for at in range(0, x.shape[1], out_cols):
        those = slice(at, at + out_cols)
        value = tn(back[...], c[:, those])
        terms[:rank, those] = scale * (value[:rank] + value[rank:])
        value = tn(low[...], x[:, those])
        terms[rank:, those] = scale * (value[:rank] + value[rank:])
    to_sibling(n_tok)
    for j in range(n_tok - 1, n_tok):
        for p in range(last):
            relay_grads(j, p)
    over_chips(n_tok - 2)
    relay_grads(1, last)
    over_core(n_tok)
    for j in range(2, n_tok):
        relay_grads(j, last)
    over_chips(n_tok - 1)
    over_chips(n_tok)
    for copy in tok_copies:
        copy.wait_recv()
    value = kept_d[0]
    for d in range(1, n_tok):
        value = value + tok_recv[d - 1].astype(F32)
    dx_out[...] = value
    value = all_t[0].astype(F32)
    for k in range(1, n_tok):
        value = value + all_t[k].astype(F32)
    terms_out[...] = value
    for j in range(n_tok):
        act_along(j, wait_send)
        for p in range(n_part):
            oa_along(j, p, wait_send)
    for groups in (from_chip, from_core, core_copies, chip_copies):
        for group in groups.values():
            for copy in group:
                copy.wait_send()
    for copy in firsts + a_core + list(weights.values()) + tok_copies:
        copy.wait_send()


def fused(n_part, scale, tokens, cotangent, frozen_in, frozen_out, in_a, in_b, out_a, out_b):
    n_tok, n_hid = lax.axis_size("tok"), lax.axis_size("hid")
    n_chip = n_hid // 2
    rows, cols = tokens.shape
    count, features = rows * n_tok, cols * n_hid
    width = frozen_in.shape[1] // n_tok
    part_width = width // n_part
    rank = in_a.shape[1]
    sems = pltpu.SemaphoreType.DMA
    vmem = pl.BlockSpec(memory_space=pltpu.VMEM)
    whole = pl.BlockSpec(memory_space=pl.ANY)
    return pl.pallas_call(
        functools.partial(fused_kernel, n_tok, n_hid, n_part, scale),
        out_shape=(
            jax.ShapeDtypeStruct((rows, cols), F32),
            jax.ShapeDtypeStruct((2 * rank, cols), F32),
            jax.ShapeDtypeStruct((n_tok * width, rank), BF16),
            jax.ShapeDtypeStruct((rank, n_tok * width), BF16),
        ),
        in_specs=[whole] * 8,
        out_specs=(vmem,) * 4,
        scratch_shapes=[
            pltpu.VMEM((count, features), BF16),
            pltpu.VMEM((count, features), BF16),
            pltpu.VMEM((features, width), BF16),
            pltpu.VMEM((width, features), BF16),
            pltpu.VMEM((features, rank), BF16),
            pltpu.VMEM((rank, features), BF16),
            pltpu.VMEM((rank, width), BF16),
            pltpu.VMEM((width, rank), BF16),
            pltpu.VMEM((2 * rank, width), BF16),
            pltpu.VMEM((width, 2 * rank), BF16),
            pltpu.VMEM((features, 2 * rank), BF16),
            pltpu.VMEM((count, 2 * rank), BF16),
            pltpu.VMEM((count, 2 * rank), BF16),
            pltpu.VMEM((rows, part_width), F32),
            pltpu.VMEM((rows, part_width), F32),
            pltpu.VMEM((rows, part_width), BF16),
            pltpu.VMEM((rows, part_width), BF16),
            pltpu.VMEM((count, features), F32),
            pltpu.VMEM((count, rank), F32),
            pltpu.VMEM((count, rank), F32),
            pltpu.VMEM((n_part, part_width, 2 * rank), F32),
            pltpu.VMEM((n_part, 2 * rank, part_width), F32),
            pltpu.VMEM((2 * rank, features), F32),
            pltpu.VMEM((n_tok, n_chip, rows, cols), F32),
            pltpu.VMEM((n_chip, 2 * rank, cols), F32),
            pltpu.VMEM((n_tok, n_chip - 1, rows, cols), BF16),
            pltpu.VMEM((n_chip - 1, 2 * rank, cols), BF16),
            pltpu.VMEM((n_tok, n_chip - 1, rows, cols), BF16),
            pltpu.VMEM((n_chip - 1, 2 * rank, cols), BF16),
            pltpu.VMEM((n_tok, rows, cols), F32),
            pltpu.VMEM((2 * rank, cols), F32),
            pltpu.VMEM((n_tok - 1, rows, cols), BF16),
            pltpu.VMEM((n_tok - 1, rows, cols), BF16),
            pltpu.VMEM((n_tok, 2 * rank, cols), BF16),
            sems((2, n_tok, 2)),
            sems((n_tok, 2)),
            sems((2, n_tok, n_chip - 1, 2)),
            sems((2, n_tok, n_chip, 2)),
            sems((2, n_chip - 1)),
            sems((2, n_chip)),
            sems((2, n_tok - 1, n_part, 2)),
            sems((6 + 2 * n_part,)),
            sems((2, n_tok + 1, n_chip)),
            sems((2, n_tok + 1, n_chip - 1)),
            sems((2, n_tok - 1)),
            sems((2, n_tok - 1)),
            sems((2, n_tok, n_part, 2)),
            sems((n_tok, n_part, 2)),
        ],
        compiler_params=pltpu.CompilerParams(
            collective_id=1, has_side_effects=True, vmem_limit_bytes=52 * 1024 * 1024
        ),
    )(tokens, cotangent, frozen_in, frozen_out, in_a, in_b, out_a, out_b)


def finish_kernel(dx, terms, oa, ib, dx_out, in_a_out, ib_out, oa_out, out_b_out):
    rank = in_a_out.shape[1]
    ib_out[...] = ib[...].astype(F32)
    oa_out[...] = oa[...].astype(F32)
    dx_out[...] = dx[...]
    in_a_out[...] = terms[rank:, :].T
    out_b_out[...] = terms[:rank, :]


def local(tokens, cotangent, frozen_in, frozen_out, in_a, in_b, out_a, out_b):
    count = tokens.shape[0] * lax.axis_size("tok")
    scale = ADAPTER_SCALE / math.sqrt(count)
    dx, terms, oa, ib = fused(
        2, scale, tokens, cotangent, frozen_in, frozen_out, in_a, in_b, out_a, out_b
    )
    rank, cols = in_a.shape[1], tokens.shape[1]
    vmem = pl.BlockSpec(memory_space=pltpu.VMEM)
    return pl.pallas_call(
        finish_kernel,
        out_shape=(
            jax.ShapeDtypeStruct(dx.shape, F32),
            jax.ShapeDtypeStruct((cols, rank), F32),
            jax.ShapeDtypeStruct(ib.shape, F32),
            jax.ShapeDtypeStruct(oa.shape, F32),
            jax.ShapeDtypeStruct((rank, cols), F32),
        ),
        in_specs=[vmem] * 4,
        out_specs=(vmem,) * 5,
        compiler_params=pltpu.CompilerParams(vmem_limit_bytes=16 * 1024 * 1024),
    )(dx, terms, oa, ib)


def local_by_rows(
    tokens,
    cotangent,
    frozen_in,
    frozen_out,
    input_adapter_first,
    input_adapter_second,
    adapter_out_a,
    adapter_out_b,
):
    highest_precision = lax.Precision.HIGHEST
    device_local_rows = tokens.shape[0]
    rank_width = input_adapter_second.shape[0]
    gradient_scale = ADAPTER_SCALE / math.sqrt(device_local_rows * lax.axis_size("tok"))
    full_tokens, full_cotan = (
        lax.all_gather(tokens, "hid", axis=1, tiled=True),
        lax.all_gather(cotangent, "hid", axis=1, tiled=True),
    )
    in_rows = lax.all_gather(frozen_in, "tok", axis=0, tiled=True)
    in_a_full = lax.all_gather(input_adapter_first, "hid", axis=0, tiled=True)
    lowrank_input = jnp.dot(full_tokens, in_a_full, preferred_element_type=jnp.float32)
    second_float = input_adapter_second.astype(jnp.float32)
    out_a_float = adapter_out_a.astype(jnp.float32)
    pre_activation = jnp.dot(
        full_tokens, in_rows, preferred_element_type=jnp.float32
    ) + ADAPTER_SCALE * jnp.dot(lowrank_input, second_float, precision=highest_precision)
    value_out, slopes = gelu_pair(pre_activation)
    hidden_act = value_out.astype(jnp.bfloat16)
    backward_lowrank = jnp.einsum(
        "td,rd->tr", full_cotan, adapter_out_b, preferred_element_type=jnp.float32
    )
    rank_out = jnp.dot(hidden_act, adapter_out_a, preferred_element_type=jnp.float32)
    dense_backward = jnp.einsum(
        "td,fd->tf",
        full_cotan,
        lax.all_gather(frozen_out, "tok", axis=1, tiled=True),
        preferred_element_type=jnp.float32,
    )
    dense_backward = dense_backward + ADAPTER_SCALE * jnp.dot(
        backward_lowrank, out_a_float.T, precision=highest_precision
    )
    grad_pre = (dense_backward * slopes).astype(jnp.bfloat16)
    rank_backward = jnp.einsum(
        "tf,rf->tr", grad_pre, input_adapter_second, preferred_element_type=jnp.float32
    )
    dense_in = jnp.einsum("tf,df->td", grad_pre, in_rows, preferred_element_type=jnp.float32)
    grad_out_a = gradient_scale * jnp.dot(
        hidden_act.astype(jnp.float32).T, backward_lowrank, precision=highest_precision
    )
    grad_in_b = gradient_scale * jnp.dot(
        lowrank_input.T, grad_pre.astype(jnp.float32), precision=highest_precision
    )
    in_a_float = in_a_full.astype(jnp.float32)
    dx_term = dense_in + ADAPTER_SCALE * jnp.dot(
        rank_backward, in_a_float.T, precision=highest_precision
    )
    out_term = jnp.dot(rank_out.T, full_cotan.astype(jnp.float32), precision=highest_precision)
    in_term = jnp.dot(rank_backward.T, full_tokens.astype(jnp.float32), precision=highest_precision)
    rank_terms = jnp.concatenate([out_term, in_term], axis=0)
    input_gradient, rank_local = (
        lax.psum_scatter(dx_term, "hid", scatter_dimension=1, tiled=True),
        lax.psum_scatter(rank_terms, "hid", scatter_dimension=1, tiled=True),
    )
    grad_out_a, grad_in_b, rank_total = lax.psum((grad_out_a, grad_in_b, rank_local), "tok")
    grad_out_b = gradient_scale * rank_total[:rank_width]
    grad_in_a = gradient_scale * rank_total[rank_width:].T
    return (input_gradient, grad_in_a, grad_in_b, grad_out_a, grad_out_b)


def solution(mesh):
    in_specs = (
        P("tok", "hid"),
        P("tok", "hid"),
        P("tok", "hid"),
        P("hid", "tok"),
        P("hid", None),
        P(None, "hid"),
        P("hid", None),
        P(),
    )
    out_specs = (P("tok", "hid"), P("hid", None), P(None, "hid"), P("hid", None), P(None, "hid"))
    def body(*arrays):
        share = arrays[2].shape[1] // lax.axis_size("tok")
        return local(*arrays) if share % 256 == 0 else local_by_rows(*arrays)

    return jax.shard_map(body, mesh=mesh, in_specs=in_specs, out_specs=out_specs, check_vma=False)
```

time: 170 us -> 129 us (0.76)
  matrix products: 30.4 us -> 0 us
  other arithmetic: 5.68 us -> 0 us
  local copies, waits for them, and re-layouts: 8.51 us -> 3.51 us
    dot_general x14 -> x0, matrix products: 30.4 us -> none  [dot(): lax.dot_general(left, right, (dims, ((), ())), preferred_element_type=F32)]
    mul x4 -> x0, other arithmetic: 4.14 us -> none  [the longest x1 1.13 us: local(): half_in_a = (ADAPTER_SCALE * in_a_full).astype(BF16)]
    unnamed x14 -> x8, local copies, waits for them, and re-layouts: 7 us -> 3.51 us
where the time goes in v1:
time: 129 us; the launch traced here: 128 us
  Pallas kernels  124 us (96%)
  local copies, waits for them, and re-layouts  3.51 us (3%)
    pallas_call x1, Pallas kernels, fused(): pl.pallas_call(functools.partial(fused_kernel, n_tok, n_hid, n_part, scal...  123 us
    unnamed x8, local copies, waits for them, and re-layouts  3.51 us

profile of v1, /device:TPU:0, one launch (start us, length us, event | category | flops | bytes accessed | tf_op | source)
XLA Modules:
  0.0 128.4 jit_solution(9540504681124045820)
XLA Ops:
  0.6 0.0 copy-start
  0.6 0.9 copy-done
  1.6 0.0 copy-start.1
  1.6 0.9 copy-done.1
  2.5 0.0 copy-start.2
  2.5 0.9 copy-done.2
  3.4 0.0 copy-start.3
  3.4 0.8 copy-done.3
  4.2 122.7 %shard_map.119 = (f32[512,128]{1,0:T(8,128)S(1)}, f32[256,128]{1,0:T(8,128)S(1)}, bf16[2048,128]{1,0:T(8,128)(2,1)S(1)}, bf16[128,2048]{1,0:T(8,128)(2,1)S(1)}) custom-call(bf16[512,128]{1,0:T(8,128)(2,1)S(1)} %copy-done.1, bf16[512,128]{1,0:T(8,128)(2,1)S(1)} %copy-done.2, bf16[256,2048]{1,0:T(8,128)(2,1)} %w_in.1, bf16[2048,256]{1,0:T(8,128)(2,1)} %w_out.1, ...), custom_call_target="tpu_custom_call" | custom-call | tf_op jit(solution)/shard_map/pallas_call | solution.py:482
  126.9 1.5 %shard_map.120 = (f32[512,128]{1,0:T(8,128)}, f32[128,128]{1,0:T(8,128)}, f32[128,2048]{1,0:T(8,128)}, f32[2048,128]{1,0:T(8,128)}, f32[128,128]{1,0:T(8,128)}) custom-call(f32[512,128]{1,0:T(8,128)S(1)} %get-tuple-element.9.dx, f32[256,128]{1,0:T(8,128)S(1)} %get-tuple-element.10.terms, bf16[2048,128]{1,0:T(8,128)(2,1)S(1)} %get-tuple-element.11.oa, ...), custom_call_target="tpu_custom_call" | custom-call | tf_op jit(solution)/shard_map/pallas_call | solution.py:565
Async XLA Ops:
  0.6 1.0 copy-start
  1.6 0.9 copy-start.1
  2.5 0.9 copy-start.2
  3.4 0.8 copy-start.3

commit v2 on v1

--- a/solution.py
+++ b/solution.py
@@ -53,9 +53,10 @@
     dx_out, terms_out, oa_all, ib_all,
     x, c, full_in, full_out, full_a, b_mat, second, first, second2, first2, a2,
     low, back, pre_s, back_s, act_s, grad_s, dense, rank_out, rank_back, oa_acc, ib_acc, terms,
-    core_d, core_t, send_d, send_t, recv_d, recv_t, kept_d, kept_t, tok_send, tok_recv, all_t,
+    core_d, core_t, kept_d, kept_t, pend_d, pend_t, one_send, one_send_t, one_recv, one_recv_t,
+    two_send, two_send_t, two_recv, two_recv_t, line_send, line_recv, all_t,
     act_send, act_recv, chip_sem, core_sem, first_sem, first_core_sem, w_sem, own_sem,
-    core_r_sem, chip_r_sem, tok_sem, term_sem, grad_send, grad_recv,
+    core_r_sem, one_sem, two_sem, line_sem, line_got, term_sem, grad_send, grad_recv,
 ):
     t, h = lax.axis_index("tok"), lax.axis_index("hid")
     n_chip = n_hid // 2
@@ -180,8 +181,11 @@
     ]
     to_core(0, 0)
     a_core = [begin(in_a, first_part(0), first_core_sem.at[0, 0], first_core_sem.at[1, 0], sibling)]
-    for d in range(1, n_tok):
-        send_weight(d, 0, 0)
+    pieces = [(d, p, k) for p in range(n_part) for k in range(2) for d in range(1, n_tok)]
+    pieces = [piece for piece in pieces if piece[1:] != (0, 0) or piece[0] in (1, n_tok - 1)]
+    rest = [(d, 0, 0) for d in range(2, n_tok - 1)] + pieces[min(2, n_tok - 1):]
+    for piece in pieces[:min(2, n_tok - 1)]:
+        send_weight(*piece)
     at = pl.multiple_of(t * width, width)
     own = [(block, target) for block, target in act_blocks(0)]
     own += [(in_a, first_part(0)), (out_b, b_mat)]
@@ -265,38 +269,43 @@
         value = nt(grad, full_in[:, those]) + nt(low[here, :], a2[...])
         dense[here, :] = dense[here, :] + value if n_part > 1 else value
 
+    def prepare():
+        for e in range(1, n_chip):
+            firsts[e - 1].wait_recv()
+            a_core.append(begin(
+                first_part(e), first_part(e), first_core_sem.at[0, e], first_core_sem.at[1, e],
+                sibling,
+            ))
+        for copy in own:
+            copy.wait()
+        for copy in a_core:
+            copy.wait_recv()
+        half = (ADAPTER_SCALE * second[...].astype(F32)).astype(BF16)
+        second2[:rank, :] = half
+        second2[rank:, :] = half
+        half = (ADAPTER_SCALE * first[...].astype(F32)).astype(BF16)
+        first2[:, :rank] = half
+        first2[:, rank:] = half
+        half = (ADAPTER_SCALE * full_a[...].astype(F32)).astype(BF16)
+        a2[:, :rank] = half
+        a2[:, rank:] = half
+
+    share = -(-len(rest) // (n_tok - 1))
     for j in range(1, n_tok):
         arrive(j)
-        if j == 1:
-            for d in range(1, n_tok):
-                send_weight(d, 0, 1)
-            for e in range(1, n_chip):
-                firsts[e - 1].wait_recv()
-                a_core.append(begin(
-                    first_part(e), first_part(e), first_core_sem.at[0, e], first_core_sem.at[1, e],
-                    sibling,
-                ))
+        for piece in rest[(j - 1) * share:j * share]:
+            send_weight(*piece)
+        if j >= 2:
+            pass_on(j - 2)
+            complete(j - 2)
         if j == n_tok - 1:
-            for p in range(1, n_part):
-                for d in range(1, n_tok):
-                    for k in range(2):
-                        send_weight(d, p, k)
-        pass_on(j - 1)
-        if j == 1:
-            for copy in own:
-                copy.wait()
-            for copy in a_core:
-                copy.wait_recv()
-            half = (ADAPTER_SCALE * second[...].astype(F32)).astype(BF16)
-            second2[:rank, :] = half
-            second2[rank:, :] = half
-            half = (ADAPTER_SCALE * first[...].astype(F32)).astype(BF16)
-            first2[:, :rank] = half
-            first2[:, rank:] = half
-            half = (ADAPTER_SCALE * full_a[...].astype(F32)).astype(BF16)
-            a2[:, :rank] = half
-            a2[:, rank:] = half
-        complete(j - 1)
+            prepare()
+        if j >= 3:
+            ranks(sources[j - 3])
+    for j in range(max(n_tok - 2, 0), n_tok):
+        if j < n_tok - 1:
+            pass_on(j)
+            complete(j)
         ranks(sources[j - 1])
 
     def wait_weights(p):
@@ -351,116 +360,173 @@
     if last > 0:
         wait_weights(last)
 
-    def block(index, parity):
-        return pl.ds(pl.multiple_of((2 * index + parity) * cols, cols), cols)
-
-    def tok_rows(d):
-        return pl.ds(row_at((t + d) % n_tok), rows)
-
-    chunks = list(range(1, n_tok)) + [0, None]
-    core_copies, chip_copies, tok_copies = {}, {}, []
+    at_x, at_y = chip % 2, chip // 2
+    square = [
+        2 * ((at_y + e // 2) % 2) + (at_x + e % 2) % 2 for e in range(n_chip)
+    ]
+    core_copies, first_copies, second_copies, tok_copies = {}, {}, {}, []
+    blocks = [sources[n_tok - 1 - q] for q in range(n_tok)]
+
+    def columns(e, parity):
+        return pl.ds(pl.multiple_of((2 * square[e] + parity) * cols, cols), cols)
+
+    def here(q):
+        return pl.ds(row_at(blocks[q]), rows)
+
+    def buffers(q):
+        if q == n_tok:
+            return core_t, kept_t, pend_t, one_send_t, one_recv_t, two_send_t, two_recv_t
+        return tuple(
+            array.at[q] for array in (core_d, kept_d, pend_d, one_send, one_recv, two_send, two_recv)
+        )
 
     def to_sibling(q):
-        d = chunks[q]
+        got = buffers(q)[0]
         core_copies[q] = []
         for e in range(n_chip):
-            columns = block((chip + e) % n_chip, 1 - core)
-            source = terms.at[:, columns] if d is None else dense.at[tok_rows(d), columns]
-            target = core_t.at[e] if d is None else core_d.at[d, e]
+            those = columns(e, 1 - core)
+            source = terms.at[:, those] if q == n_tok else dense.at[here(q), those]
             core_copies[q].append(
-                begin(source, target, core_r_sem.at[0, q, e], core_r_sem.at[1, q, e], sibling)
+                begin(source, got.at[e], core_r_sem.at[0, q, e], core_r_sem.at[1, q, e], sibling)
             )
 
     def over_core(q):
-        d = chunks[q]
-        chip_copies[q] = []
-        for e in list(range(1, n_chip)) + [0]:
+        got, kept, pend, sent, recv = buffers(q)[:5]
+        half = kept.shape[0] // 2
+        first_copies[q] = []
+        for e in (3, 1, 2, 0):
             core_copies[q][e].wait_recv()
-            columns = block((chip + e) % n_chip, core)
-            if d is None:
-                value = terms[:, columns] + core_t[e]
-            else:
-                value = dense[tok_rows(d), columns] + core_d[d, e]
-            if e == 0:
-                if d is None:
-                    kept_t[...] = value
+            those = columns(e, core)
+            mine = terms[:, those] if q == n_tok else dense[here(q), those]
+            value = mine + got[e]
+            for i in range(2):
+                some = value[i * half:(i + 1) * half]
+                if e == 0:
+                    kept[i * half:(i + 1) * half, :] = some
+                elif e == 2 - i:
+                    pend[i] = some
                 else:
-                    kept_d[d] = value
-                continue
-            sent, got = (send_t, recv_t) if d is None else (send_d.at[d], recv_d.at[d])
-            sent[e - 1] = value.astype(BF16)
-            chip_copies[q].append(begin(
-                sent.at[e - 1], got.at[e - 1],
-                chip_r_sem.at[0, q, e - 1], chip_r_sem.at[1, q, e - 1], chips[e],
+                    sent[i, 0 if e == 1 + i else 1] = some.astype(BF16)
+        for i in range(2):
+            first_copies[q].append(begin(
+                sent.at[i], recv.at[i], one_sem.at[0, q, i], one_sem.at[1, q, i],
+                (t, 2 * square[1 + i] + core),
             ))
 
-    def over_chips(q):
-        d = chunks[q]
-        for copy in chip_copies[q]:
-            copy.wait_recv()
-        got = recv_t if d is None else recv_d.at[d]
-        value = kept_t[...] if d is None else kept_d[d]
-        for e in range(n_chip - 1):
-            value = value + got[e].astype(F32)
-        if d is None:
-            all_t[t] = value.astype(BF16)
-            for k in range(1, n_tok):
-                tok_copies.append(begin(
-                    all_t.at[t], all_t.at[t], term_sem.at[0, k - 1], term_sem.at[1, k - 1], toks[k]
-                ))
-        elif d == 0:
-            kept_d[0] = value
-        else:
-            tok_send[d - 1] = value.astype(BF16)
+    def over_first(q):
+        _, kept, pend, _, recv, sent, second_recv = buffers(q)
+        half = kept.shape[0] // 2
+        second_copies[q] = []
+        for i in range(2):
+            first_copies[q][i].wait_recv()
+            sent[i] = (pend[i] + recv[i, 1].astype(F32)).astype(BF16)
+            second_copies[q].append(begin(
+                sent.at[i], second_recv.at[i], two_sem.at[0, q, i], two_sem.at[1, q, i],
+                (t, 2 * square[2 - i] + core),
+            ))
+            some = slice(i * half, (i + 1) * half)
+            kept[some, :] = kept[some, :] + recv[i, 0].astype(F32)
+
+    def over_second(q):
+        _, kept, _, _, _, _, recv = buffers(q)
+        half = kept.shape[0] // 2
+        for i in range(2):
+            second_copies[q][i].wait_recv()
+            some = slice(i * half, (i + 1) * half)
+            kept[some, :] = kept[some, :] + recv[i].astype(F32)
+
+    def line_copy(q, way):
+        where = (t + 1 - 2 * way, h)
+        return remote(
+            line_send.at[min(q, n_tok - 2)], line_recv.at[way, blocks[q]],
+            line_sem.at[way, min(q, n_tok - 2)], line_got.at[way, blocks[q]], where,
+        )
+
+    def from_line(q, way):
+        line_copy(q, way).wait_recv()
+        kept_d[q] = kept_d[q] + line_recv[way, blocks[q]].astype(F32)
+
+    def over_line(q):
+        target = blocks[q]
+        pl.when((target >= t) & (t > 0))(lambda: from_line(q, 0))
+        pl.when((target <= t) & (t + 1 < n_tok))(lambda: from_line(q, 1))
+        if q == n_tok - 1:
+            return
+        line_send[q] = kept_d[q].astype(BF16)
+        pl.when(target > t)(lambda: line_copy(q, 0).start())
+        pl.when(target < t)(lambda: line_copy(q, 1).start())
+
+    def share_terms():
+        all_t[t] = kept_t[...].astype(BF16)
+        for k in range(1, n_tok):
             tok_copies.append(begin(
-                tok_send.at[d - 1], tok_recv.at[d - 1],
-                tok_sem.at[0, d - 1], tok_sem.at[1, d - 1], toks[d],
+                all_t.at[t], all_t.at[t], term_sem.at[0, k - 1], term_sem.at[1, k - 1], toks[k]
             ))
 
+    def sum_terms():
+        out_cols = x.shape[1] // n_chip
+        for at in range(0, x.shape[1], out_cols):
+            those = slice(at, at + out_cols)
+            value = tn(back[...], c[:, those])
+            terms[:rank, those] = scale * (value[:rank] + value[rank:])
+            value = tn(low[...], x[:, those])
+            terms[rank:, those] = scale * (value[:rank] + value[rank:])
+
+    def relay_all(j):
+        for p in range(last):
+            relay_grads(j, p)
+
+    final = n_tok - 1
     for q in range(n_tok):
-        hidden(last, (t + chunks[q]) % n_tok, q > 0)
+        hidden(last, blocks[q], q > 0)
         to_sibling(q)
         if q >= 1:
             over_core(q - 1)
         if q >= 2:
-            over_chips(q - 2)
-            for p in range(last):
-                relay_grads(q - 1, p)
+            relay_all(q - 1)
+        if q >= 3:
+            over_first(q - 3)
     finish_grads(last)
-    over_core(n_tok - 1)
-    out_cols = x.shape[1] // n_chip
-    for at in range(0, x.shape[1], out_cols):
-        those = slice(at, at + out_cols)
-        value = tn(back[...], c[:, those])
-        terms[:rank, those] = scale * (value[:rank] + value[rank:])
-        value = tn(low[...], x[:, those])
-        terms[rank:, those] = scale * (value[:rank] + value[rank:])
+    over_first(final - 2)
+    sum_terms()
     to_sibling(n_tok)
-    for j in range(n_tok - 1, n_tok):
-        for p in range(last):
-            relay_grads(j, p)
-    over_chips(n_tok - 2)
+    for j in range(max(n_tok - 1, 1), n_tok):
+        relay_all(j)
+    for q in range(final - 2):
+        over_second(q)
+        over_line(q)
+    over_first(final - 1)
+    over_core(n_tok)
+    over_second(final - 2)
+    over_line(final - 2)
+    over_core(final)
     relay_grads(1, last)
-    over_core(n_tok)
-    for j in range(2, n_tok):
+    over_first(n_tok)
+    over_second(final - 1)
+    over_line(final - 1)
+    over_first(final)
+    over_second(n_tok)
+    share_terms()
+    relay_grads(2, last)
+    over_second(final)
+    for j in range(3, n_tok):
         relay_grads(j, last)
-    over_chips(n_tok - 1)
-    over_chips(n_tok)
+    over_line(final)
+    dx_out[...] = kept_d[final]
     for copy in tok_copies:
         copy.wait_recv()
-    value = kept_d[0]
-    for d in range(1, n_tok):
-        value = value + tok_recv[d - 1].astype(F32)
-    dx_out[...] = value
     value = all_t[0].astype(F32)
     for k in range(1, n_tok):
         value = value + all_t[k].astype(F32)
     terms_out[...] = value
+    for q in range(final):
+        pl.when(blocks[q] > t)(lambda: line_copy(q, 0).wait_send())
+        pl.when(blocks[q] < t)(lambda: line_copy(q, 1).wait_send())
     for j in range(n_tok):
         act_along(j, wait_send)
         for p in range(n_part):
             oa_along(j, p, wait_send)
-    for groups in (from_chip, from_core, core_copies, chip_copies):
+    for groups in (from_chip, from_core, core_copies, first_copies, second_copies):
         for group in groups.values():
             for copy in group:
                 copy.wait_send()
@@ -515,14 +581,20 @@
             pltpu.VMEM((2 * rank, features), F32),
             pltpu.VMEM((n_tok, n_chip, rows, cols), F32),
             pltpu.VMEM((n_chip, 2 * rank, cols), F32),
-            pltpu.VMEM((n_tok, n_chip - 1, rows, cols), BF16),
-            pltpu.VMEM((n_chip - 1, 2 * rank, cols), BF16),
-            pltpu.VMEM((n_tok, n_chip - 1, rows, cols), BF16),
-            pltpu.VMEM((n_chip - 1, 2 * rank, cols), BF16),
             pltpu.VMEM((n_tok, rows, cols), F32),
             pltpu.VMEM((2 * rank, cols), F32),
+            pltpu.VMEM((n_tok, 2, rows // 2, cols), F32),
+            pltpu.VMEM((2, rank, cols), F32),
+            pltpu.VMEM((n_tok, 2, 2, rows // 2, cols), BF16),
+            pltpu.VMEM((2, 2, rank, cols), BF16),
+            pltpu.VMEM((n_tok, 2, 2, rows // 2, cols), BF16),
+            pltpu.VMEM((2, 2, rank, cols), BF16),
+            pltpu.VMEM((n_tok, 2, rows // 2, cols), BF16),
+            pltpu.VMEM((2, rank, cols), BF16),
+            pltpu.VMEM((n_tok, 2, rows // 2, cols), BF16),
+            pltpu.VMEM((2, rank, cols), BF16),
             pltpu.VMEM((n_tok - 1, rows, cols), BF16),
-            pltpu.VMEM((n_tok - 1, rows, cols), BF16),
+            pltpu.VMEM((2, n_tok, rows, cols), BF16),
             pltpu.VMEM((n_tok, 2 * rank, cols), BF16),
             sems((2, n_tok, 2)),
             sems((n_tok, 2)),
@@ -533,14 +605,16 @@
             sems((2, n_tok - 1, n_part, 2)),
             sems((6 + 2 * n_part,)),
             sems((2, n_tok + 1, n_chip)),
-            sems((2, n_tok + 1, n_chip - 1)),
+            sems((2, n_tok + 1, 2)),
+            sems((2, n_tok + 1, 2)),
             sems((2, n_tok - 1)),
+            sems((2, n_tok)),
             sems((2, n_tok - 1)),
             sems((2, n_tok, n_part, 2)),
             sems((n_tok, n_part, 2)),
         ],
         compiler_params=pltpu.CompilerParams(
-            collective_id=1, has_side_effects=True, vmem_limit_bytes=52 * 1024 * 1024
+            collective_id=1, has_side_effects=True, vmem_limit_bytes=60 * 1024 * 1024
         ),
     )(tokens, cotangent, frozen_in, frozen_out, in_a, in_b, out_a, out_b)
 
@@ -573,7 +647,7 @@
         ),
         in_specs=[vmem] * 4,
         out_specs=(vmem,) * 5,
-        compiler_params=pltpu.CompilerParams(vmem_limit_bytes=16 * 1024 * 1024),
+        compiler_params=pltpu.CompilerParams(vmem_limit_bytes=60 * 1024 * 1024),
     )(dx, terms, oa, ib)
 
 
@@ -660,6 +734,8 @@
     out_specs = (P("tok", "hid"), P("hid", None), P(None, "hid"), P("hid", None), P(None, "hid"))
     def body(*arrays):
         share = arrays[2].shape[1] // lax.axis_size("tok")
-        return local(*arrays) if share % 256 == 0 else local_by_rows(*arrays)
+        wide = share % 256 == 0 and lax.axis_size("tok") > 2
+        wide = wide and lax.axis_size("hid") == 2 ** len(("y", "x", "core"))
+        return local(*arrays) if wide else local_by_rows(*arrays)
 
     return jax.shard_map(body, mesh=mesh, in_specs=in_specs, out_specs=out_specs, check_vma=False)

time: 129 us -> 127 us (0.984)
  local copies, waits for them, and re-layouts: 3.51 us -> 0 us
  Pallas kernels: 124 us -> 126 us
    unnamed x8 -> x0, local copies, waits for them, and re-layouts: 3.51 us -> none
    pallas_call x1, Pallas kernels: 1.54 us -> 2.89 us  [local(): pl.pallas_call(finish_kernel, out_shape=(jax.ShapeDtypeStruct(dx.shape, F...]
where the time goes in v2:
time: 127 us
  Pallas kernels  126 us (99%)
    pallas_call x1, Pallas kernels, fused(): pl.pallas_call(functools.partial(fused_kernel, n_tok, n_hid, n_part, scal...  124 us
    pallas_call x1, Pallas kernels, local(): pl.pallas_call(finish_kernel, out_shape=(jax.ShapeDtypeStruct(dx.shape, F...  2.89 us

profile of v2, /device:TPU:0, one launch (start us, length us, event | category | flops | bytes accessed | tf_op | source)
XLA Modules:
  0.0 127.1 jit_solution(5208152912062772006)
XLA Ops:
  0.6 123.5 %shard_map.119 = (f32[512,128]{1,0:T(8,128)}, f32[256,128]{1,0:T(8,128)}, bf16[2048,128]{1,0:T(8,128)(2,1)}, bf16[128,2048]{1,0:T(8,128)(2,1)}) custom-call(bf16[512,128]{1,0:T(8,128)(2,1)} %tokens.1, bf16[512,128]{1,0:T(8,128)(2,1)} %cotangent.1, bf16[256,2048]{1,0:T(8,128)(2,1)} %w_in.1, bf16[2048,256]{1,0:T(8,128)(2,1)} %w_out.1, bf16[128,128]{1,0:T(8,128)(2,1)} %in_a.1, ...), custom_call_target="tpu_custom_call" | custom-call | tf_op jit(solution)/shard_map/pallas_call | solution.py:548
  124.2 2.9 %shard_map.120 = (f32[512,128]{1,0:T(8,128)}, f32[128,128]{1,0:T(8,128)}, f32[128,2048]{1,0:T(8,128)}, f32[2048,128]{1,0:T(8,128)}, f32[128,128]{1,0:T(8,128)}) custom-call(f32[512,128]{1,0:T(8,128)} %get-tuple-element.9.dx, f32[256,128]{1,0:T(8,128)} %get-tuple-element.10.terms, bf16[2048,128]{1,0:T(8,128)(2,1)} %get-tuple-element.11.oa, ...), custom_call_target="tpu_custom_call" | custom-call | tf_op jit(solution)/shard_map/pallas_call | solution.py:639

commit v3 on v2

--- a/solution.py
+++ b/solution.py
@@ -290,10 +290,10 @@
         a2[:, :rank] = half
         a2[:, rank:] = half
 
-    share = -(-len(rest) // (n_tok - 1))
+    early = len(pieces) // 3
     for j in range(1, n_tok):
         arrive(j)
-        for piece in rest[(j - 1) * share:j * share]:
+        for piece in {2: rest[:early], n_tok - 1: rest[early:]}.get(j, []):
             send_weight(*piece)
         if j >= 2:
             pass_on(j - 2)
@@ -318,9 +318,9 @@
         oa_at, ib_at = oa_all.at[pl.ds(at, part_width), :], ib_all.at[:, pl.ds(at, part_width)]
         return [(oa_at, oa_at), (ib_at, ib_at)]
 
-    def oa_along(j, p, act):
+    def grads_along(source, p, act):
         along(
-            sources[j], oa_blocks(sources[j], p),
+            source, oa_blocks(source, p),
             lambda way, source, k: grad_send.at[way, source, p, k],
             lambda source, k: grad_recv.at[source, p, k], act,
         )
@@ -331,15 +331,20 @@
         oa_all[pl.ds(at, part_width), :] = (scale * (oa[:, :rank] + oa[:, rank:])).astype(BF16)
         ib = ib_acc[p]
         ib_all[:, pl.ds(at, part_width)] = (scale * (ib[:rank] + ib[rank:])).astype(BF16)
-        oa_along(0, p, start)
-
-    def relay_grads(j, p):
-        for k, (block, target) in enumerate(oa_blocks(sources[j], p)):
-            remote(
-                target, target, grad_send.at[0, sources[j], p, k], grad_recv.at[sources[j], p, k],
-                sibling,
-            ).wait_recv()
-        oa_along(j, p, start)
+        grads_along(t, p, start)
+
+    def grad_hop(s, p):
+        def relay(source):
+            blocks = oa_blocks(source, p)
+            for k, (block, target) in enumerate(blocks):
+                remote(
+                    target, target, grad_send.at[0, source, p, k], grad_recv.at[source, p, k],
+                    sibling,
+                ).wait_recv()
+            grads_along(source, p, start)
+
+        pl.when(t >= s + 1)(lambda: relay(t - 1 - s))
+        pl.when(t + 1 + s < n_tok)(lambda: relay(t + 1 + s))
 
     wait_weights(0)
     if n_part > 1:
@@ -472,9 +477,9 @@
             value = tn(low[...], x[:, those])
             terms[rank:, those] = scale * (value[:rank] + value[rank:])
 
-    def relay_all(j):
+    def hop(s):
         for p in range(last):
-            relay_grads(j, p)
+            grad_hop(s, p)
 
     final = n_tok - 1
     for q in range(n_tok):
@@ -482,35 +487,32 @@
         to_sibling(q)
         if q >= 1:
             over_core(q - 1)
-        if q >= 2:
-            relay_all(q - 1)
-        if q >= 3:
-            over_first(q - 3)
+        if q == 2:
+            hop(0)
     finish_grads(last)
-    over_first(final - 2)
+    for q in range(final - 1):
+        over_first(q)
     sum_terms()
     to_sibling(n_tok)
-    for j in range(max(n_tok - 1, 1), n_tok):
-        relay_all(j)
-    for q in range(final - 2):
+    hop(1)
+    over_core(n_tok)
+    over_first(final - 1)
+    over_core(final)
+    for q in range(final - 1):
         over_second(q)
         over_line(q)
-    over_first(final - 1)
-    over_core(n_tok)
-    over_second(final - 2)
-    over_line(final - 2)
-    over_core(final)
-    relay_grads(1, last)
+    grad_hop(0, last)
     over_first(n_tok)
     over_second(final - 1)
     over_line(final - 1)
     over_first(final)
     over_second(n_tok)
     share_terms()
-    relay_grads(2, last)
+    for s in range(2, n_tok - 1):
+        hop(s)
     over_second(final)
-    for j in range(3, n_tok):
-        relay_grads(j, last)
+    for s in range(1, n_tok - 1):
+        grad_hop(s, last)
     over_line(final)
     dx_out[...] = kept_d[final]
     for copy in tok_copies:
@@ -525,7 +527,7 @@
     for j in range(n_tok):
         act_along(j, wait_send)
         for p in range(n_part):
-            oa_along(j, p, wait_send)
+            grads_along(sources[j], p, wait_send)
     for groups in (from_chip, from_core, core_copies, first_copies, second_copies):
         for group in groups.values():
             for copy in group:

time: 127 us -> 111 us (0.87)
  Pallas kernels: 126 us -> 110 us
    pallas_call x1, Pallas kernels: 124 us -> 107 us  [fused(): pl.pallas_call(functools.partial(fused_kernel, n_tok, n_hid, n_part, scal...]
where the time goes in v3:
time: 111 us; the launch traced here: 110 us
  Pallas kernels  110 us (99%)
    pallas_call x1, Pallas kernels, fused(): pl.pallas_call(functools.partial(fused_kernel, n_tok, n_hid, n_part, scal...  107 us
    pallas_call x1, Pallas kernels, local(): pl.pallas_call(finish_kernel, out_shape=(jax.ShapeDtypeStruct(dx.shape, F...  2.89 us

profile of v3, /device:TPU:0, one launch (start us, length us, event | category | flops | bytes accessed | tf_op | source)
XLA Modules:
  0.0 110.4 jit_solution(12640096957173630615)
XLA Ops:
  0.6 106.9 %shard_map.119 = (f32[512,128]{1,0:T(8,128)}, f32[256,128]{1,0:T(8,128)}, bf16[2048,128]{1,0:T(8,128)(2,1)}, bf16[128,2048]{1,0:T(8,128)(2,1)}) custom-call(bf16[512,128]{1,0:T(8,128)(2,1)} %tokens.1, bf16[512,128]{1,0:T(8,128)(2,1)} %cotangent.1, bf16[256,2048]{1,0:T(8,128)(2,1)} %w_in.1, bf16[2048,256]{1,0:T(8,128)(2,1)} %w_out.1, bf16[128,128]{1,0:T(8,128)(2,1)} %in_a.1, ...), custom_call_target="tpu_custom_call" | custom-call | tf_op jit(solution)/shard_map/pallas_call | solution.py:550
  107.5 2.9 %shard_map.120 = (f32[512,128]{1,0:T(8,128)}, f32[128,128]{1,0:T(8,128)}, f32[128,2048]{1,0:T(8,128)}, f32[2048,128]{1,0:T(8,128)}, f32[128,128]{1,0:T(8,128)}) custom-call(f32[512,128]{1,0:T(8,128)} %get-tuple-element.9.dx, f32[256,128]{1,0:T(8,128)} %get-tuple-element.10.terms, bf16[2048,128]{1,0:T(8,128)(2,1)} %get-tuple-element.11.oa, ...), custom_call_target="tpu_custom_call" | custom-call | tf_op jit(solution)/shard_map/pallas_call | solution.py:641

commit v4 on v3

--- a/solution.py
+++ b/solution.py
@@ -86,7 +86,10 @@
         pl.semaphore_signal(barrier, inc=1, device_id=where, device_id_type=pl.DeviceIdType.MESH)
     pl.semaphore_wait(barrier, n_chip + n_tok - 1)
 
-    orders = [sorted(range(n_tok), key=lambda s: (abs(s - k), s)) for k in range(n_tok)]
+    orders = [
+        sorted(range(n_tok), key=lambda s: (abs(s - k), -abs(2 * s - n_tok + 1)))
+        for k in range(n_tok)
+    ]
     sources = [t]
     for j in range(1, n_tok):
         source = jnp.int32(orders[0][j])
@@ -447,19 +450,25 @@
             line_sem.at[way, min(q, n_tok - 2)], line_got.at[way, blocks[q]], where,
         )
 
-    def from_line(q, way):
+    def send_line(q, way):
+        line_send[q] = kept_d[q].astype(BF16)
+        line_copy(q, way).start()
+
+    def add_line(q, way):
         line_copy(q, way).wait_recv()
         kept_d[q] = kept_d[q] + line_recv[way, blocks[q]].astype(F32)
 
+    def start_line(q):
+        pl.when((blocks[q] > t) & (t == 0))(lambda: send_line(q, 0))
+        pl.when((blocks[q] < t) & (t == n_tok - 1))(lambda: send_line(q, 1))
+
     def over_line(q):
-        target = blocks[q]
-        pl.when((target >= t) & (t > 0))(lambda: from_line(q, 0))
-        pl.when((target <= t) & (t + 1 < n_tok))(lambda: from_line(q, 1))
-        if q == n_tok - 1:
-            return
-        line_send[q] = kept_d[q].astype(BF16)
-        pl.when(target > t)(lambda: line_copy(q, 0).start())
-        pl.when(target < t)(lambda: line_copy(q, 1).start())
+        def add_and_send(way):
+            add_line(q, way)
+            send_line(q, way)
+
+        pl.when((blocks[q] > t) & (t > 0))(lambda: add_and_send(0))
+        pl.when((blocks[q] < t) & (t < n_tok - 1))(lambda: add_and_send(1))
 
     def share_terms():
         all_t[t] = kept_t[...].astype(BF16)
@@ -497,23 +506,31 @@
     hop(1)
     over_core(n_tok)
     over_first(final - 1)
+    over_second(0)
+    start_line(0)
+    grad_hop(0, last)
+    for q in range(1, final - 1):
+        over_second(q)
+        start_line(q)
+    over_first(n_tok)
     over_core(final)
-    for q in range(final - 1):
-        over_second(q)
-        over_line(q)
-    grad_hop(0, last)
-    over_first(n_tok)
+    over_line(0)
     over_second(final - 1)
-    over_line(final - 1)
-    over_first(final)
+    start_line(final - 1)
     over_second(n_tok)
     share_terms()
+    if n_tok > 2:
+        grad_hop(1, last)
+    over_first(final)
+    for q in range(1, final):
+        over_line(q)
     for s in range(2, n_tok - 1):
         hop(s)
     over_second(final)
-    for s in range(1, n_tok - 1):
+    for s in range(2, n_tok - 1):
         grad_hop(s, last)
-    over_line(final)
+    pl.when(t > 0)(lambda: add_line(final, 0))
+    pl.when(t < n_tok - 1)(lambda: add_line(final, 1))
     dx_out[...] = kept_d[final]
     for copy in tok_copies:
         copy.wait_recv()
@@ -547,6 +564,7 @@
     sems = pltpu.SemaphoreType.DMA
     vmem = pl.BlockSpec(memory_space=pltpu.VMEM)
     whole = pl.BlockSpec(memory_space=pl.ANY)
+    arguments = (tokens, cotangent, frozen_in, frozen_out, in_a, in_b, out_a, out_b)
     return pl.pallas_call(
         functools.partial(fused_kernel, n_tok, n_hid, n_part, scale),
         out_shape=(
@@ -616,9 +634,9 @@
             sems((n_tok, n_part, 2)),
         ],
         compiler_params=pltpu.CompilerParams(
-            collective_id=1, has_side_effects=True, vmem_limit_bytes=60 * 1024 * 1024
+            collective_id=1, has_side_effects=True, vmem_limit_bytes=52 * 1024 * 1024
         ),
-    )(tokens, cotangent, frozen_in, frozen_out, in_a, in_b, out_a, out_b)
+    )(*(pltpu.with_memory_space_constraint(array, pltpu.HBM) for array in arguments))
 
 
 def finish_kernel(dx, terms, oa, ib, dx_out, in_a_out, ib_out, oa_out, out_b_out):
@@ -649,7 +667,7 @@
         ),
         in_specs=[vmem] * 4,
         out_specs=(vmem,) * 5,
-        compiler_params=pltpu.CompilerParams(vmem_limit_bytes=60 * 1024 * 1024),
+        compiler_params=pltpu.CompilerParams(vmem_limit_bytes=16 * 1024 * 1024),
     )(dx, terms, oa, ib)
 
 

time: 111 us -> 104 us (0.937)
  Pallas kernels: 110 us -> 103 us
    pallas_call x1, Pallas kernels: 107 us -> 101 us  [fused(): pl.pallas_call(functools.partial(fused_kernel, n_tok, n_hid, n_part, scal...]
    pallas_call x1, Pallas kernels: 2.89 us -> 1.54 us  [local(): pl.pallas_call(finish_kernel, out_shape=(jax.ShapeDtypeStruct(dx.shape, F...]
where the time goes in v4:
time: 104 us
  Pallas kernels  103 us (99%)
    pallas_call x1, Pallas kernels, fused(): pl.pallas_call(functools.partial(fused_kernel, n_tok, n_hid, n_part, scal...  101 us

profile of v4, /device:TPU:0, one launch (start us, length us, event | category | flops | bytes accessed | tf_op | source)
XLA Modules:
  0.0 103.5 jit_solution(9155424681139454723)
XLA Ops:
  0.6 101.3 %shard_map.119 = (f32[512,128]{1,0:T(8,128)S(1)}, f32[256,128]{1,0:T(8,128)S(1)}, bf16[2048,128]{1,0:T(8,128)(2,1)S(1)}, bf16[128,2048]{1,0:T(8,128)(2,1)S(1)}) custom-call(bf16[512,128]{1,0:T(8,128)(2,1)} %tokens.1, bf16[512,128]{1,0:T(8,128)(2,1)} %cotangent.1, bf16[256,2048]{1,0:T(8,128)(2,1)} %w_in.1, bf16[2048,256]{1,0:T(8,128)(2,1)} %w_out.1, ...), custom_call_target="tpu_custom_call" | custom-call | tf_op jit(solution)/shard_map/pallas_call | solution.py:568
  102.0 1.5 %shard_map.120 = (f32[512,128]{1,0:T(8,128)}, f32[128,128]{1,0:T(8,128)}, f32[128,2048]{1,0:T(8,128)}, f32[2048,128]{1,0:T(8,128)}, f32[128,128]{1,0:T(8,128)}) custom-call(f32[512,128]{1,0:T(8,128)S(1)} %get-tuple-element.9.dx, f32[256,128]{1,0:T(8,128)S(1)} %get-tuple-element.10.terms, bf16[2048,128]{1,0:T(8,128)(2,1)S(1)} %get-tuple-element.11.oa, ...), custom_call_target="tpu_custom_call" | custom-call | tf_op jit(solution)/shard_map/pallas_call | solution.py:659

commit v5 on v4

--- a/solution.py
+++ b/solution.py
@@ -52,7 +52,7 @@
     tokens, cotangent, w_in, w_out, in_a, in_b, out_a, out_b,
     dx_out, terms_out, oa_all, ib_all,
     x, c, full_in, full_out, full_a, b_mat, second, first, second2, first2, a2,
-    low, back, pre_s, back_s, act_s, grad_s, dense, rank_out, rank_back, oa_acc, ib_acc, terms,
+    low, back, outs, pre_s, slopes, act_s, grad_s, dense, rank_out, rank_back, oa_acc, ib_acc, terms,
     core_d, core_t, kept_d, kept_t, pend_d, pend_t, one_send, one_send_t, one_recv, one_recv_t,
     two_send, two_send_t, two_recv, two_recv_t, line_send, line_recv, all_t,
     act_send, act_recv, chip_sem, core_sem, first_sem, first_core_sem, w_sem, own_sem,
@@ -231,46 +231,49 @@
         back[here, :rank] = high
         back[here, rank:] = rest
 
-    def hidden(p, source, begun):
+    def forward(p, source, begun):
         here = pl.ds(row_at(source), rows)
         those = slice(p * part_width, (p + 1) * part_width)
         pre_s[...] = nn(x[here, :], full_in[:, those]) + nn(low[here, :], second2[:, those])
-        back_s[...] = nt(c[here, :], full_out[those, :]) + nt(back[here, :], first2[those, :])
         step = rows // 8
         for at in range(0, rows, step):
             some = slice(at, at + step)
-            value_out, slopes = gelu_pair(pre_s[some, :])
+            value_out, slope = gelu_pair(pre_s[some, :])
             act_s[some, :] = value_out.astype(BF16)
-            grad_s[some, :] = (back_s[some, :] * slopes).astype(BF16)
-        act, grad = act_s[...], grad_s[...]
-        oa_new, ib_new = tn(act, back[here, :]), tn(low[here, :], grad)
-        out_new, back_new = nn(act, first[those, :]), nt(grad, second[:, those])
-        if begun:
-            oa_acc[p] += oa_new
-            ib_acc[p] += ib_new
+            slopes[pl.ds(pl.multiple_of(row_at(source) + at, step), step), :] = slope
+        act = act_s[...]
+        oa_new, out_new = tn(act, back[here, :]), nn(act, first[those, :])
+        oa_acc[p] = oa_acc[p] + oa_new if begun else oa_new
+        value = out_new if p == 0 else rank_out[here, :] + out_new
+        if p < n_part - 1:
+            rank_out[here, :] = value
         else:
-            oa_acc[p] = oa_new
-            ib_acc[p] = ib_new
-        if p == 0:
-            rank_out[here, :] = out_new
-            rank_back[here, :] = back_new
+            high, rest = split(value)
+            outs[here, :rank] = high
+            outs[here, rank:] = rest
+
+    def backward(p, source, begun):
+        here = pl.ds(row_at(source), rows)
+        those = slice(p * part_width, (p + 1) * part_width)
+        value = nt(c[here, :], full_out[those, :]) + nt(back[here, :], first2[those, :])
+        grad_s[...] = (value * slopes[here, :]).astype(BF16)
+        grad = grad_s[...]
+        ib_new, back_new = tn(low[here, :], grad), nt(grad, second[:, those])
+        ib_acc[p] = ib_acc[p] + ib_new if begun else ib_new
+        value = back_new if p == 0 else rank_back[here, :] + back_new
+        if p < n_part - 1:
+            rank_back[here, :] = value
+            value = nt(grad, full_in[:, those])
         else:
-            rank_out[here, :] += out_new
-            rank_back[here, :] += back_new
-        if p < n_part - 1:
-            if p == 0:
-                dense[here, :] = nt(grad, full_in[:, those])
-            else:
-                dense[here, :] += nt(grad, full_in[:, those])
-            return
-        high, rest = split(rank_back[here, :])
-        low[here, :rank] = high
-        low[here, rank:] = rest
-        high, rest = split(rank_out[here, :])
-        back[here, :rank] = high
-        back[here, rank:] = rest
-        value = nt(grad, full_in[:, those]) + nt(low[here, :], a2[...])
-        dense[here, :] = dense[here, :] + value if n_part > 1 else value
+            high, rest = split(value)
+            low[here, :rank] = high
+            low[here, rank:] = rest
+            value = nt(grad, full_in[:, those]) + nt(low[here, :], a2[...])
+        dense[here, :] = value if p == 0 else dense[here, :] + value
+
+    def hidden(p, source, begun):
+        forward(p, source, begun)
+        backward(p, source, begun)
 
     def prepare():
         for e in range(1, n_chip):
@@ -311,62 +314,62 @@
             complete(j)
         ranks(sources[j - 1])
 
-    def wait_weights(p):
+    def wait_weights(p, k):
         for d in range(1, n_tok):
-            for k in range(2):
-                weights[d, p, k].wait_recv()
-
-    def oa_blocks(source, p):
+            weights[d, p, k].wait_recv()
+
+    def grad_block(source, p, k):
         at = pl.multiple_of(source * width + p * part_width, part_width)
-        oa_at, ib_at = oa_all.at[pl.ds(at, part_width), :], ib_all.at[:, pl.ds(at, part_width)]
-        return [(oa_at, oa_at), (ib_at, ib_at)]
-
-    def grads_along(source, p, act):
+        if k == 0:
+            return oa_all.at[pl.ds(at, part_width), :]
+        return ib_all.at[:, pl.ds(at, part_width)]
+
+    def grads_along(source, p, k, act):
+        block = grad_block(source, p, k)
         along(
-            source, oa_blocks(source, p),
-            lambda way, source, k: grad_send.at[way, source, p, k],
-            lambda source, k: grad_recv.at[source, p, k], act,
+            source, [(block, block)],
+            lambda way, source, _: grad_send.at[way, source, p, k],
+            lambda source, _: grad_recv.at[source, p, k], act,
         )
 
-    def finish_grads(p):
-        at = pl.multiple_of(t * width + p * part_width, part_width)
-        oa = oa_acc[p]
-        oa_all[pl.ds(at, part_width), :] = (scale * (oa[:, :rank] + oa[:, rank:])).astype(BF16)
-        ib = ib_acc[p]
-        ib_all[:, pl.ds(at, part_width)] = (scale * (ib[:rank] + ib[rank:])).astype(BF16)
-        grads_along(t, p, start)
-
-    def grad_hop(s, p):
+    def finish_grad(p, k):
+        block = grad_block(t, p, k)
+        if k == 0:
+            value = oa_acc[p]
+            value = value[:, :rank] + value[:, rank:]
+        else:
+            value = ib_acc[p]
+            value = value[:rank] + value[rank:]
+        block[...] = (scale * value).astype(BF16)
+        grads_along(t, p, k, start)
+
+    def grad_hop(s, p, k):
         def relay(source):
-            blocks = oa_blocks(source, p)
-            for k, (block, target) in enumerate(blocks):
-                remote(
-                    target, target, grad_send.at[0, source, p, k], grad_recv.at[source, p, k],
-                    sibling,
-                ).wait_recv()
-            grads_along(source, p, start)
+            block = grad_block(source, p, k)
+            remote(
+                block, block, grad_send.at[0, source, p, k], grad_recv.at[source, p, k], sibling
+            ).wait_recv()
+            grads_along(source, p, k, start)
 
         pl.when(t >= s + 1)(lambda: relay(t - 1 - s))
         pl.when(t + 1 + s < n_tok)(lambda: relay(t + 1 + s))
 
-    wait_weights(0)
-    if n_part > 1:
-        for j in range(n_tok - 1):
-            hidden(0, sources[j], j > 0)
-    pass_on(n_tok - 1)
-    complete(n_tok - 1)
-    ranks(sources[n_tok - 1])
-    if n_part > 1:
-        hidden(0, sources[n_tok - 1], True)
-        finish_grads(0)
-    for p in range(1, n_part - 1):
-        wait_weights(p)
+    last = n_part - 1
+    for p in range(last):
+        for k in range(2):
+            wait_weights(p, k)
         for j in range(n_tok):
+            if p == 0 and j == n_tok - 1:
+                pass_on(j)
+                complete(j)
+                ranks(sources[j])
             hidden(p, sources[j], j > 0)
-        finish_grads(p)
-    last = n_part - 1
-    if last > 0:
-        wait_weights(last)
+        for k in range(2):
+            finish_grad(p, k)
+    wait_weights(last, 0)
+    for j in range(n_tok):
+        forward(last, sources[j], j > 0)
+    finish_grad(last, 0)
 
     at_x, at_y = chip % 2, chip // 2
     square = [
@@ -382,8 +385,10 @@
         return pl.ds(row_at(blocks[q]), rows)
 
     def buffers(q):
-        if q == n_tok:
-            return core_t, kept_t, pend_t, one_send_t, one_recv_t, two_send_t, two_recv_t
+        if q >= n_tok:
+            return tuple(array.at[q - n_tok] for array in (
+                core_t, kept_t, pend_t, one_send_t, one_recv_t, two_send_t, two_recv_t
+            ))
         return tuple(
             array.at[q] for array in (core_d, kept_d, pend_d, one_send, one_recv, two_send, two_recv)
         )
@@ -393,7 +398,7 @@
         core_copies[q] = []
         for e in range(n_chip):
             those = columns(e, 1 - core)
-            source = terms.at[:, those] if q == n_tok else dense.at[here(q), those]
+            source = terms.at[q - n_tok, :, those] if q >= n_tok else dense.at[here(q), those]
             core_copies[q].append(
                 begin(source, got.at[e], core_r_sem.at[0, q, e], core_r_sem.at[1, q, e], sibling)
             )
@@ -405,7 +410,7 @@
         for e in (3, 1, 2, 0):
             core_copies[q][e].wait_recv()
             those = columns(e, core)
-            mine = terms[:, those] if q == n_tok else dense[here(q), those]
+            mine = terms[q - n_tok, :, those] if q >= n_tok else dense[here(q), those]
             value = mine + got[e]
             for i in range(2):
                 some = value[i * half:(i + 1) * half]
@@ -470,57 +475,68 @@
         pl.when((blocks[q] > t) & (t > 0))(lambda: add_and_send(0))
         pl.when((blocks[q] < t) & (t < n_tok - 1))(lambda: add_and_send(1))
 
-    def share_terms():
-        all_t[t] = kept_t[...].astype(BF16)
+    def share_terms(i):
+        all_t[i, t] = kept_t[i].astype(BF16)
         for k in range(1, n_tok):
             tok_copies.append(begin(
-                all_t.at[t], all_t.at[t], term_sem.at[0, k - 1], term_sem.at[1, k - 1], toks[k]
+                all_t.at[i, t], all_t.at[i, t],
+                term_sem.at[0, k - 1, i], term_sem.at[1, k - 1, i], toks[k],
             ))
 
-    def sum_terms():
+    def sum_terms(i):
+        ranks_of, of = ((outs, c), (low, x))[i]
         out_cols = x.shape[1] // n_chip
         for at in range(0, x.shape[1], out_cols):
             those = slice(at, at + out_cols)
-            value = tn(back[...], c[:, those])
-            terms[:rank, those] = scale * (value[:rank] + value[rank:])
-            value = tn(low[...], x[:, those])
-            terms[rank:, those] = scale * (value[:rank] + value[rank:])
+            value = tn(ranks_of[...], of[:, those])
+            terms[i, :, those] = scale * (value[:rank] + value[rank:])
+
+    early = [(p, k) for p in range(last) for k in range(2)] + [(last, 0)]
 
     def hop(s):
-        for p in range(last):
-            grad_hop(s, p)
-
-    final = n_tok - 1
+        for p, k in early:
+            grad_hop(s, p, k)
+
+    final, out_term, in_term = n_tok - 1, n_tok, n_tok + 1
+    sum_terms(0)
+    to_sibling(out_term)
+    over_core(out_term)
+    wait_weights(last, 1)
     for q in range(n_tok):
-        hidden(last, blocks[q], q > 0)
+        backward(last, blocks[q], q > 0)
         to_sibling(q)
+        if q == 0:
+            over_first(out_term)
         if q >= 1:
             over_core(q - 1)
+        if q == 1:
+            over_second(out_term)
+            share_terms(0)
         if q == 2:
             hop(0)
-    finish_grads(last)
+    finish_grad(last, 1)
+    sum_terms(1)
+    to_sibling(in_term)
     for q in range(final - 1):
         over_first(q)
-    sum_terms()
-    to_sibling(n_tok)
+    over_core(in_term)
     hop(1)
-    over_core(n_tok)
     over_first(final - 1)
     over_second(0)
     start_line(0)
-    grad_hop(0, last)
+    grad_hop(0, last, 1)
     for q in range(1, final - 1):
         over_second(q)
         start_line(q)
-    over_first(n_tok)
+    over_first(in_term)
     over_core(final)
     over_line(0)
     over_second(final - 1)
     start_line(final - 1)
-    over_second(n_tok)
-    share_terms()
+    over_second(in_term)
+    share_terms(1)
     if n_tok > 2:
-        grad_hop(1, last)
+        grad_hop(1, last, 1)
     over_first(final)
     for q in range(1, final):
         over_line(q)
@@ -528,23 +544,25 @@
         hop(s)
     over_second(final)
     for s in range(2, n_tok - 1):
-        grad_hop(s, last)
+        grad_hop(s, last, 1)
     pl.when(t > 0)(lambda: add_line(final, 0))
     pl.when(t < n_tok - 1)(lambda: add_line(final, 1))
     dx_out[...] = kept_d[final]
     for copy in tok_copies:
         copy.wait_recv()
-    value = all_t[0].astype(F32)
-    for k in range(1, n_tok):
-        value = value + all_t[k].astype(F32)
-    terms_out[...] = value
+    for i in range(2):
+        value = all_t[i, 0].astype(F32)
+        for k in range(1, n_tok):
+            value = value + all_t[i, k].astype(F32)
+        terms_out[i * rank:(i + 1) * rank, :] = value
     for q in range(final):
         pl.when(blocks[q] > t)(lambda: line_copy(q, 0).wait_send())
         pl.when(blocks[q] < t)(lambda: line_copy(q, 1).wait_send())
     for j in range(n_tok):
         act_along(j, wait_send)
         for p in range(n_part):
-            grads_along(sources[j], p, wait_send)
+            for k in range(2):
+                grads_along(sources[j], p, k, wait_send)
     for groups in (from_chip, from_core, core_copies, first_copies, second_copies):
         for group in groups.values():
             for copy in group:
@@ -589,8 +607,9 @@
             pltpu.VMEM((features, 2 * rank), BF16),
             pltpu.VMEM((count, 2 * rank), BF16),
             pltpu.VMEM((count, 2 * rank), BF16),
+            pltpu.VMEM((count, 2 * rank), BF16),
             pltpu.VMEM((rows, part_width), F32),
-            pltpu.VMEM((rows, part_width), F32),
+            pltpu.VMEM((count, part_width), F32),
             pltpu.VMEM((rows, part_width), BF16),
             pltpu.VMEM((rows, part_width), BF16),
             pltpu.VMEM((count, features), F32),
@@ -598,24 +617,24 @@
             pltpu.VMEM((count, rank), F32),
             pltpu.VMEM((n_part, part_width, 2 * rank), F32),
             pltpu.VMEM((n_part, 2 * rank, part_width), F32),
-            pltpu.VMEM((2 * rank, features), F32),
+            pltpu.VMEM((2, rank, features), F32),
             pltpu.VMEM((n_tok, n_chip, rows, cols), F32),
-            pltpu.VMEM((n_chip, 2 * rank, cols), F32),
+            pltpu.VMEM((2, n_chip, rank, cols), F32),
             pltpu.VMEM((n_tok, rows, cols), F32),
-            pltpu.VMEM((2 * rank, cols), F32),
+            pltpu.VMEM((2, rank, cols), F32),
             pltpu.VMEM((n_tok, 2, rows // 2, cols), F32),
-            pltpu.VMEM((2, rank, cols), F32),
+            pltpu.VMEM((2, 2, rank // 2, cols), F32),
             pltpu.VMEM((n_tok, 2, 2, rows // 2, cols), BF16),
-            pltpu.VMEM((2, 2, rank, cols), BF16),
+            pltpu.VMEM((2, 2, 2, rank // 2, cols), BF16),
             pltpu.VMEM((n_tok, 2, 2, rows // 2, cols), BF16),
-            pltpu.VMEM((2, 2, rank, cols), BF16),
+            pltpu.VMEM((2, 2, 2, rank // 2, cols), BF16),
             pltpu.VMEM((n_tok, 2, rows // 2, cols), BF16),
-            pltpu.VMEM((2, rank, cols), BF16),
+            pltpu.VMEM((2, 2, rank // 2, cols), BF16),
             pltpu.VMEM((n_tok, 2, rows // 2, cols), BF16),
-            pltpu.VMEM((2, rank, cols), BF16),
+            pltpu.VMEM((2, 2, rank // 2, cols), BF16),
             pltpu.VMEM((n_tok - 1, rows, cols), BF16),
             pltpu.VMEM((2, n_tok, rows, cols), BF16),
-            pltpu.VMEM((n_tok, 2 * rank, cols), BF16),
+            pltpu.VMEM((2, n_tok, rank, cols), BF16),
             sems((2, n_tok, 2)),
             sems((n_tok, 2)),
             sems((2, n_tok, n_chip - 1, 2)),
@@ -624,12 +643,12 @@
             sems((2, n_chip)),
             sems((2, n_tok - 1, n_part, 2)),
             sems((6 + 2 * n_part,)),
-            sems((2, n_tok + 1, n_chip)),
-            sems((2, n_tok + 1, 2)),
-            sems((2, n_tok + 1, 2)),
+            sems((2, n_tok + 2, n_chip)),
+            sems((2, n_tok + 2, 2)),
+            sems((2, n_tok + 2, 2)),
             sems((2, n_tok - 1)),
             sems((2, n_tok)),
-            sems((2, n_tok - 1)),
+            sems((2, n_tok - 1, 2)),
             sems((2, n_tok, n_part, 2)),
             sems((n_tok, n_part, 2)),
         ],

time: 104 us -> 110 us (1.058)
  Pallas kernels: 103 us -> 110 us
    pallas_call x1, Pallas kernels: 101 us -> 108 us  [fused(): pl.pallas_call(functools.partial(fused_kernel, n_tok, n_hid, n_part, scal...]
where the time goes in v5:
time: 110 us
  Pallas kernels  110 us (100%)
    pallas_call x1, Pallas kernels, fused(): pl.pallas_call(functools.partial(fused_kernel, n_tok, n_hid, n_part, scal...  108 us

profile of v5, /device:TPU:0, one launch (start us, length us, event | category | flops | bytes accessed | tf_op | source)
XLA Modules:
  0.0 110.3 jit_solution(6586212764575009493)
XLA Ops:
  0.6 108.1 %shard_map.119 = (f32[512,128]{1,0:T(8,128)S(1)}, f32[256,128]{1,0:T(8,128)S(1)}, bf16[2048,128]{1,0:T(8,128)(2,1)S(1)}, bf16[128,2048]{1,0:T(8,128)(2,1)S(1)}) custom-call(bf16[512,128]{1,0:T(8,128)(2,1)} %tokens.1, bf16[512,128]{1,0:T(8,128)(2,1)} %cotangent.1, bf16[256,2048]{1,0:T(8,128)(2,1)} %w_in.1, bf16[2048,256]{1,0:T(8,128)(2,1)} %w_out.1, ...), custom_call_target="tpu_custom_call" | custom-call | tf_op jit(solution)/shard_map/pallas_call | solution.py:586
  108.8 1.5 %shard_map.120 = (f32[512,128]{1,0:T(8,128)}, f32[128,128]{1,0:T(8,128)}, f32[128,2048]{1,0:T(8,128)}, f32[2048,128]{1,0:T(8,128)}, f32[128,128]{1,0:T(8,128)}) custom-call(f32[512,128]{1,0:T(8,128)S(1)} %get-tuple-element.9.dx, f32[256,128]{1,0:T(8,128)S(1)} %get-tuple-element.10.terms, bf16[2048,128]{1,0:T(8,128)(2,1)S(1)} %get-tuple-element.11.oa, ...), custom_call_target="tpu_custom_call" | custom-call | tf_op jit(solution)/shard_map/pallas_call | solution.py:678

commit v6 on v4

--- a/solution.py
+++ b/solution.py
@@ -54,9 +54,9 @@
     x, c, full_in, full_out, full_a, b_mat, second, first, second2, first2, a2,
     low, back, pre_s, back_s, act_s, grad_s, dense, rank_out, rank_back, oa_acc, ib_acc, terms,
     core_d, core_t, kept_d, kept_t, pend_d, pend_t, one_send, one_send_t, one_recv, one_recv_t,
-    two_send, two_send_t, two_recv, two_recv_t, line_send, line_recv, all_t,
+    two_send, two_send_t, two_recv, two_recv_t, line_send, line_recv, pair_recv, all_t,
     act_send, act_recv, chip_sem, core_sem, first_sem, first_core_sem, w_sem, own_sem,
-    core_r_sem, one_sem, two_sem, line_sem, line_got, term_sem, grad_send, grad_recv,
+    core_r_sem, one_sem, two_sem, line_sem, line_got, pair_sem, term_sem, grad_send, grad_recv,
 ):
     t, h = lax.axis_index("tok"), lax.axis_index("hid")
     n_chip = n_hid // 2
@@ -78,6 +78,10 @@
         copy.start()
         return copy
 
+    at_x, at_y = chip % 2, chip // 2
+    square = [
+        2 * ((at_y + e // 2) % 2) + (at_x + e % 2) % 2 for e in range(n_chip)
+    ]
     sibling = (t, 2 * chip + 1 - core)
     chips = [(t, 2 * ((chip + e) % n_chip) + core) for e in range(n_chip)]
     toks = [((t + d) % n_tok, h) for d in range(n_tok)]
@@ -100,9 +104,11 @@
     def row_at(source):
         return pl.multiple_of(source * rows, rows)
 
-    def part(array, source, e):
-        at_col = pl.multiple_of((2 * ((chip + n_chip - e) % n_chip) + core) * cols, cols)
-        return array.at[pl.ds(row_at(source), rows), pl.ds(at_col, cols)]
+    def part(array, source, e, i=None):
+        at_col = pl.multiple_of((2 * square[e] + core) * cols, cols)
+        count = rows if i is None else rows // 2
+        at_row = pl.multiple_of(row_at(source) + (i or 0) * count, count)
+        return array.at[pl.ds(at_row, count), pl.ds(at_col, cols)]
 
     def along(source, blocks, send, recv, act):
         @pl.when((source <= t) & (t + 1 < n_tok))
@@ -139,9 +145,12 @@
     from_chip, from_core = {}, {}
 
     def to_chips(j):
-        for e in range(1, n_chip):
+        for e in (1, 2):
             from_chip[j, e] = [
-                begin(block, target, chip_sem.at[0, j, e - 1, k], chip_sem.at[1, j, e - 1, k], chips[e])
+                begin(
+                    block, target, chip_sem.at[0, j, e - 1, k], chip_sem.at[1, j, e - 1, k],
+                    (t, 2 * square[e] + core),
+                )
                 for k, (block, target) in enumerate(act_blocks(j))
             ]
 
@@ -211,11 +220,25 @@
         to_chips(j)
         to_core(j, 0)
 
-    def pass_on(j):
-        for e in range(1, n_chip):
+    def near(j):
+        for e in (1, 2):
             for copy in from_chip[j, e]:
                 copy.wait_recv()
+            from_chip[j, 2 + e] = [
+                begin(
+                    part(array, sources[j], e, e - 1), part(array, sources[j], e, e - 1),
+                    chip_sem.at[0, j, 1 + e, k], chip_sem.at[1, j, 1 + e, k],
+                    (t, 2 * square[3 - e] + core),
+                )
+                for k, array in enumerate((x, c))
+            ]
             to_core(j, e)
+
+    def far(j):
+        for e in (3, 4):
+            for copy in from_chip[j, e]:
+                copy.wait_recv()
+        to_core(j, 3)
 
     def complete(j):
         for e in range(n_chip):
@@ -294,22 +317,28 @@
         a2[:, rank:] = half
 
     early = len(pieces) // 3
-    for j in range(1, n_tok):
-        arrive(j)
+
+    def more(j):
         for piece in {2: rest[:early], n_tok - 1: rest[early:]}.get(j, []):
             send_weight(*piece)
-        if j >= 2:
-            pass_on(j - 2)
-            complete(j - 2)
-        if j == n_tok - 1:
-            prepare()
-        if j >= 3:
-            ranks(sources[j - 3])
-    for j in range(max(n_tok - 2, 0), n_tok):
-        if j < n_tok - 1:
-            pass_on(j)
-            complete(j)
-        ranks(sources[j - 1])
+
+    for j in range(1, n_tok - 1):
+        arrive(j)
+        more(j)
+    near(0)
+    arrive(n_tok - 1)
+    more(n_tok - 1)
+    far(0)
+    near(1)
+    complete(0)
+    prepare()
+    ranks(sources[0])
+    for j in range(1, n_tok - 1):
+        far(j)
+        near(j + 1)
+        complete(j)
+        ranks(sources[j])
+    far(n_tok - 1)
 
     def wait_weights(p):
         for d in range(1, n_tok):
@@ -349,29 +378,16 @@
         pl.when(t >= s + 1)(lambda: relay(t - 1 - s))
         pl.when(t + 1 + s < n_tok)(lambda: relay(t + 1 + s))
 
-    wait_weights(0)
-    if n_part > 1:
-        for j in range(n_tok - 1):
-            hidden(0, sources[j], j > 0)
-    pass_on(n_tok - 1)
     complete(n_tok - 1)
     ranks(sources[n_tok - 1])
-    if n_part > 1:
-        hidden(0, sources[n_tok - 1], True)
-        finish_grads(0)
-    for p in range(1, n_part - 1):
+    for p in range(n_part - 1):
         wait_weights(p)
         for j in range(n_tok):
             hidden(p, sources[j], j > 0)
         finish_grads(p)
     last = n_part - 1
-    if last > 0:
-        wait_weights(last)
-
-    at_x, at_y = chip % 2, chip // 2
-    square = [
-        2 * ((at_y + e // 2) % 2) + (at_x + e % 2) % 2 for e in range(n_chip)
-    ]
+    wait_weights(last)
+
     core_copies, first_copies, second_copies, tok_copies = {}, {}, {}, []
     blocks = [sources[n_tok - 1 - q] for q in range(n_tok)]
 
@@ -443,32 +459,48 @@
             some = slice(i * half, (i + 1) * half)
             kept[some, :] = kept[some, :] + recv[i].astype(F32)
 
-    def line_copy(q, way):
-        where = (t + 1 - 2 * way, h)
+    at_end = (t == 0) | (t == n_tok - 1)
+
+    def pair_copy():
         return remote(
-            line_send.at[min(q, n_tok - 2)], line_recv.at[way, blocks[q]],
-            line_sem.at[way, min(q, n_tok - 2)], line_got.at[way, blocks[q]], where,
+            line_send.at[0], pair_recv, pair_sem.at[0], pair_sem.at[1],
+            (jnp.where(t == 0, 1, n_tok - 2), h),
         )
 
-    def send_line(q, way):
+    def line_copy(q):
+        return remote(
+            line_send.at[q], line_recv.at[t], line_sem.at[q], line_got.at[t], (blocks[q], h)
+        )
+
+    def send_line(q):
         line_send[q] = kept_d[q].astype(BF16)
-        line_copy(q, way).start()
-
-    def add_line(q, way):
-        line_copy(q, way).wait_recv()
-        kept_d[q] = kept_d[q] + line_recv[way, blocks[q]].astype(F32)
-
-    def start_line(q):
-        pl.when((blocks[q] > t) & (t == 0))(lambda: send_line(q, 0))
-        pl.when((blocks[q] < t) & (t == n_tok - 1))(lambda: send_line(q, 1))
-
-    def over_line(q):
-        def add_and_send(way):
-            add_line(q, way)
-            send_line(q, way)
-
-        pl.when((blocks[q] > t) & (t > 0))(lambda: add_and_send(0))
-        pl.when((blocks[q] < t) & (t < n_tok - 1))(lambda: add_and_send(1))
+        line_copy(q).start()
+
+    def start_pair():
+        def send():
+            line_send[0] = kept_d[0].astype(BF16)
+            pair_copy().start()
+
+        pl.when(at_end)(send)
+
+    def over_pair():
+        def add_and_send():
+            pair_copy().wait_recv()
+            kept_d[0] = kept_d[0] + pair_recv[...].astype(F32)
+            send_line(0)
+
+        pl.when(jnp.logical_not(at_end))(add_and_send)
+
+    def add_line(source):
+        def add():
+            remote(
+                line_recv.at[source], line_recv.at[source], line_sem.at[0], line_got.at[source],
+                sibling,
+            ).wait_recv()
+            kept_d[n_tok - 1] = kept_d[n_tok - 1] + line_recv[source].astype(F32)
+
+        far = (t + source == n_tok - 1) & at_end
+        pl.when((t != source) & jnp.logical_not(far))(add)
 
     def share_terms():
         all_t[t] = kept_t[...].astype(BF16)
@@ -507,30 +539,28 @@
     over_core(n_tok)
     over_first(final - 1)
     over_second(0)
-    start_line(0)
+    start_pair()
     grad_hop(0, last)
     for q in range(1, final - 1):
         over_second(q)
-        start_line(q)
+        send_line(q)
     over_first(n_tok)
     over_core(final)
-    over_line(0)
+    over_pair()
     over_second(final - 1)
-    start_line(final - 1)
+    send_line(final - 1)
     over_second(n_tok)
     share_terms()
     if n_tok > 2:
         grad_hop(1, last)
     over_first(final)
-    for q in range(1, final):
-        over_line(q)
     for s in range(2, n_tok - 1):
         hop(s)
     over_second(final)
     for s in range(2, n_tok - 1):
         grad_hop(s, last)
-    pl.when(t > 0)(lambda: add_line(final, 0))
-    pl.when(t < n_tok - 1)(lambda: add_line(final, 1))
+    for source in range(n_tok):
+        add_line(source)
     dx_out[...] = kept_d[final]
     for copy in tok_copies:
         copy.wait_recv()
@@ -538,9 +568,10 @@
     for k in range(1, n_tok):
         value = value + all_t[k].astype(F32)
     terms_out[...] = value
-    for q in range(final):
-        pl.when(blocks[q] > t)(lambda: line_copy(q, 0).wait_send())
-        pl.when(blocks[q] < t)(lambda: line_copy(q, 1).wait_send())
+    pl.when(at_end)(lambda: pair_copy().wait_send())
+    pl.when(jnp.logical_not(at_end))(lambda: line_copy(0).wait_send())
+    for q in range(1, final):
+        line_copy(q).wait_send()
     for j in range(n_tok):
         act_along(j, wait_send)
         for p in range(n_part):
@@ -614,11 +645,12 @@
             pltpu.VMEM((n_tok, 2, rows // 2, cols), BF16),
             pltpu.VMEM((2, rank, cols), BF16),
             pltpu.VMEM((n_tok - 1, rows, cols), BF16),
-            pltpu.VMEM((2, n_tok, rows, cols), BF16),
+            pltpu.VMEM((n_tok, rows, cols), BF16),
+            pltpu.VMEM((rows, cols), BF16),
             pltpu.VMEM((n_tok, 2 * rank, cols), BF16),
             sems((2, n_tok, 2)),
             sems((n_tok, 2)),
-            sems((2, n_tok, n_chip - 1, 2)),
+            sems((2, n_tok, 4, 2)),
             sems((2, n_tok, n_chip, 2)),
             sems((2, n_chip - 1)),
             sems((2, n_chip)),
@@ -627,8 +659,9 @@
             sems((2, n_tok + 1, n_chip)),
             sems((2, n_tok + 1, 2)),
             sems((2, n_tok + 1, 2)),
-            sems((2, n_tok - 1)),
-            sems((2, n_tok)),
+            sems((n_tok - 1,)),
+            sems((n_tok,)),
+            sems((2,)),
             sems((2, n_tok - 1)),
             sems((2, n_tok, n_part, 2)),
             sems((n_tok, n_part, 2)),
@@ -754,7 +787,7 @@
     out_specs = (P("tok", "hid"), P("hid", None), P(None, "hid"), P("hid", None), P(None, "hid"))
     def body(*arrays):
         share = arrays[2].shape[1] // lax.axis_size("tok")
-        wide = share % 256 == 0 and lax.axis_size("tok") > 2
+        wide = share % 256 == 0 and lax.axis_size("tok") == lax.axis_size("hid") // 2
         wide = wide and lax.axis_size("hid") == 2 ** len(("y", "x", "core"))
         return local(*arrays) if wide else local_by_rows(*arrays)
 

time: 104 us -> 107 us (1.029)
  Pallas kernels: 103 us -> 106 us
    pallas_call x1, Pallas kernels: 101 us -> 104 us  [fused(): pl.pallas_call(functools.partial(fused_kernel, n_tok, n_hid, n_part, scal...]
where the time goes in v6:
time: 107 us; the launch traced here: 106 us
  Pallas kernels  106 us (99%)
    pallas_call x1, Pallas kernels, fused(): pl.pallas_call(functools.partial(fused_kernel, n_tok, n_hid, n_part, scal...  104 us

profile of v6, /device:TPU:0, one launch (start us, length us, event | category | flops | bytes accessed | tf_op | source)
XLA Modules:
  0.0 106.5 jit_solution(5555015415818297857)
XLA Ops:
  0.6 104.3 %shard_map.119 = (f32[512,128]{1,0:T(8,128)S(1)}, f32[256,128]{1,0:T(8,128)S(1)}, bf16[2048,128]{1,0:T(8,128)(2,1)S(1)}, bf16[128,2048]{1,0:T(8,128)(2,1)S(1)}) custom-call(bf16[512,128]{1,0:T(8,128)(2,1)} %tokens.1, bf16[512,128]{1,0:T(8,128)(2,1)} %cotangent.1, bf16[256,2048]{1,0:T(8,128)(2,1)} %w_in.1, bf16[2048,256]{1,0:T(8,128)(2,1)} %w_out.1, ...), custom_call_target="tpu_custom_call" | custom-call | tf_op jit(solution)/shard_map/pallas_call | solution.py:599
  104.9 1.5 %shard_map.120 = (f32[512,128]{1,0:T(8,128)}, f32[128,128]{1,0:T(8,128)}, f32[128,2048]{1,0:T(8,128)}, f32[2048,128]{1,0:T(8,128)}, f32[128,128]{1,0:T(8,128)}) custom-call(f32[512,128]{1,0:T(8,128)S(1)} %get-tuple-element.9.dx, f32[256,128]{1,0:T(8,128)S(1)} %get-tuple-element.10.terms, bf16[2048,128]{1,0:T(8,128)(2,1)S(1)} %get-tuple-element.11.oa, ...), custom_call_target="tpu_custom_call" | custom-call | tf_op jit(solution)/shard_map/pallas_call | solution.py:692

commit v7 on v6

--- a/solution.py
+++ b/solution.py
@@ -54,9 +54,9 @@
     x, c, full_in, full_out, full_a, b_mat, second, first, second2, first2, a2,
     low, back, pre_s, back_s, act_s, grad_s, dense, rank_out, rank_back, oa_acc, ib_acc, terms,
     core_d, core_t, kept_d, kept_t, pend_d, pend_t, one_send, one_send_t, one_recv, one_recv_t,
-    two_send, two_send_t, two_recv, two_recv_t, line_send, line_recv, pair_recv, all_t,
+    two_send, two_send_t, two_recv, two_recv_t, line_send, line_recv, all_t,
     act_send, act_recv, chip_sem, core_sem, first_sem, first_core_sem, w_sem, own_sem,
-    core_r_sem, one_sem, two_sem, line_sem, line_got, pair_sem, term_sem, grad_send, grad_recv,
+    core_r_sem, one_sem, two_sem, line_sem, line_got, term_sem, grad_send, grad_recv,
 ):
     t, h = lax.axis_index("tok"), lax.axis_index("hid")
     n_chip = n_hid // 2
@@ -459,48 +459,32 @@
             some = slice(i * half, (i + 1) * half)
             kept[some, :] = kept[some, :] + recv[i].astype(F32)
 
-    at_end = (t == 0) | (t == n_tok - 1)
-
-    def pair_copy():
+    def line_copy(q, way):
+        where = (t + 1 - 2 * way, h)
         return remote(
-            line_send.at[0], pair_recv, pair_sem.at[0], pair_sem.at[1],
-            (jnp.where(t == 0, 1, n_tok - 2), h),
+            line_send.at[min(q, n_tok - 2)], line_recv.at[way, blocks[q]],
+            line_sem.at[way, min(q, n_tok - 2)], line_got.at[way, blocks[q]], where,
         )
 
-    def line_copy(q):
-        return remote(
-            line_send.at[q], line_recv.at[t], line_sem.at[q], line_got.at[t], (blocks[q], h)
-        )
-
-    def send_line(q):
+    def send_line(q, way):
         line_send[q] = kept_d[q].astype(BF16)
-        line_copy(q).start()
-
-    def start_pair():
-        def send():
-            line_send[0] = kept_d[0].astype(BF16)
-            pair_copy().start()
-
-        pl.when(at_end)(send)
-
-    def over_pair():
-        def add_and_send():
-            pair_copy().wait_recv()
-            kept_d[0] = kept_d[0] + pair_recv[...].astype(F32)
-            send_line(0)
-
-        pl.when(jnp.logical_not(at_end))(add_and_send)
-
-    def add_line(source):
-        def add():
-            remote(
-                line_recv.at[source], line_recv.at[source], line_sem.at[0], line_got.at[source],
-                sibling,
-            ).wait_recv()
-            kept_d[n_tok - 1] = kept_d[n_tok - 1] + line_recv[source].astype(F32)
-
-        far = (t + source == n_tok - 1) & at_end
-        pl.when((t != source) & jnp.logical_not(far))(add)
+        line_copy(q, way).start()
+
+    def add_line(q, way):
+        line_copy(q, way).wait_recv()
+        kept_d[q] = kept_d[q] + line_recv[way, blocks[q]].astype(F32)
+
+    def start_line(q):
+        pl.when((blocks[q] > t) & (t == 0))(lambda: send_line(q, 0))
+        pl.when((blocks[q] < t) & (t == n_tok - 1))(lambda: send_line(q, 1))
+
+    def over_line(q):
+        def add_and_send(way):
+            add_line(q, way)
+            send_line(q, way)
+
+        pl.when((blocks[q] > t) & (t > 0))(lambda: add_and_send(0))
+        pl.when((blocks[q] < t) & (t < n_tok - 1))(lambda: add_and_send(1))
 
     def share_terms():
         all_t[t] = kept_t[...].astype(BF16)
@@ -531,36 +515,38 @@
         if q == 2:
             hop(0)
     finish_grads(last)
+    sum_terms()
+    to_sibling(n_tok)
     for q in range(final - 1):
         over_first(q)
-    sum_terms()
-    to_sibling(n_tok)
+    over_core(n_tok)
     hop(1)
-    over_core(n_tok)
     over_first(final - 1)
     over_second(0)
-    start_pair()
+    start_line(0)
     grad_hop(0, last)
     for q in range(1, final - 1):
         over_second(q)
-        send_line(q)
+        start_line(q)
     over_first(n_tok)
     over_core(final)
-    over_pair()
+    over_line(0)
     over_second(final - 1)
-    send_line(final - 1)
+    start_line(final - 1)
     over_second(n_tok)
     share_terms()
     if n_tok > 2:
         grad_hop(1, last)
     over_first(final)
+    for q in range(1, final):
+        over_line(q)
     for s in range(2, n_tok - 1):
         hop(s)
     over_second(final)
     for s in range(2, n_tok - 1):
         grad_hop(s, last)
-    for source in range(n_tok):
-        add_line(source)
+    pl.when(t > 0)(lambda: add_line(final, 0))
+    pl.when(t < n_tok - 1)(lambda: add_line(final, 1))
     dx_out[...] = kept_d[final]
     for copy in tok_copies:
         copy.wait_recv()
@@ -568,10 +554,9 @@
     for k in range(1, n_tok):
         value = value + all_t[k].astype(F32)
     terms_out[...] = value
-    pl.when(at_end)(lambda: pair_copy().wait_send())
-    pl.when(jnp.logical_not(at_end))(lambda: line_copy(0).wait_send())
-    for q in range(1, final):
-        line_copy(q).wait_send()
+    for q in range(final):
+        pl.when(blocks[q] > t)(lambda: line_copy(q, 0).wait_send())
+        pl.when(blocks[q] < t)(lambda: line_copy(q, 1).wait_send())
     for j in range(n_tok):
         act_along(j, wait_send)
         for p in range(n_part):
@@ -645,8 +630,7 @@
             pltpu.VMEM((n_tok, 2, rows // 2, cols), BF16),
             pltpu.VMEM((2, rank, cols), BF16),
             pltpu.VMEM((n_tok - 1, rows, cols), BF16),
-            pltpu.VMEM((n_tok, rows, cols), BF16),
-            pltpu.VMEM((rows, cols), BF16),
+            pltpu.VMEM((2, n_tok, rows, cols), BF16),
             pltpu.VMEM((n_tok, 2 * rank, cols), BF16),
             sems((2, n_tok, 2)),
             sems((n_tok, 2)),
@@ -659,9 +643,8 @@
             sems((2, n_tok + 1, n_chip)),
             sems((2, n_tok + 1, 2)),
             sems((2, n_tok + 1, 2)),
-            sems((n_tok - 1,)),
-            sems((n_tok,)),
-            sems((2,)),
+            sems((2, n_tok - 1)),
+            sems((2, n_tok)),
             sems((2, n_tok - 1)),
             sems((2, n_tok, n_part, 2)),
             sems((n_tok, n_part, 2)),
@@ -787,7 +770,7 @@
     out_specs = (P("tok", "hid"), P("hid", None), P(None, "hid"), P("hid", None), P(None, "hid"))
     def body(*arrays):
         share = arrays[2].shape[1] // lax.axis_size("tok")
-        wide = share % 256 == 0 and lax.axis_size("tok") == lax.axis_size("hid") // 2
+        wide = share % 256 == 0 and lax.axis_size("tok") > 2
         wide = wide and lax.axis_size("hid") == 2 ** len(("y", "x", "core"))
         return local(*arrays) if wide else local_by_rows(*arrays)
 

time: 107 us -> 104 us (0.972)
  Pallas kernels: 106 us -> 103 us
    pallas_call x1, Pallas kernels: 104 us -> 101 us  [fused(): pl.pallas_call(functools.partial(fused_kernel, n_tok, n_hid, n_part, scal...]
where the time goes in v7:
time: 104 us; the launch traced here: 103 us
  Pallas kernels  103 us (99%)
    pallas_call x1, Pallas kernels, fused(): pl.pallas_call(functools.partial(fused_kernel, n_tok, n_hid, n_part, scal...  101 us

profile of v7, /device:TPU:0, one launch (start us, length us, event | category | flops | bytes accessed | tf_op | source)
XLA Modules:
  0.0 103.5 jit_solution(8148387681461816372)
XLA Ops:
  0.6 101.3 %shard_map.119 = (f32[512,128]{1,0:T(8,128)S(1)}, f32[256,128]{1,0:T(8,128)S(1)}, bf16[2048,128]{1,0:T(8,128)(2,1)S(1)}, bf16[128,2048]{1,0:T(8,128)(2,1)S(1)}) custom-call(bf16[512,128]{1,0:T(8,128)(2,1)} %tokens.1, bf16[512,128]{1,0:T(8,128)(2,1)} %cotangent.1, bf16[256,2048]{1,0:T(8,128)(2,1)} %w_in.1, bf16[2048,256]{1,0:T(8,128)(2,1)} %w_out.1, ...), custom_call_target="tpu_custom_call" | custom-call | tf_op jit(solution)/shard_map/pallas_call | solution.py:584
  101.9 1.5 %shard_map.120 = (f32[512,128]{1,0:T(8,128)}, f32[128,128]{1,0:T(8,128)}, f32[128,2048]{1,0:T(8,128)}, f32[2048,128]{1,0:T(8,128)}, f32[128,128]{1,0:T(8,128)}) custom-call(f32[512,128]{1,0:T(8,128)S(1)} %get-tuple-element.9.dx, f32[256,128]{1,0:T(8,128)S(1)} %get-tuple-element.10.terms, bf16[2048,128]{1,0:T(8,128)(2,1)S(1)} %get-tuple-element.11.oa, ...), custom_call_target="tpu_custom_call" | custom-call | tf_op jit(solution)/shard_map/pallas_call | solution.py:675

commit v8 on v7

--- a/solution.py
+++ b/solution.py
@@ -459,20 +459,37 @@
             some = slice(i * half, (i + 1) * half)
             kept[some, :] = kept[some, :] + recv[i].astype(F32)
 
-    def line_copy(q, way):
+    def half_rows(i):
+        return pl.ds(i * (rows // 2), rows // 2)
+
+    def line_copy(q, way, i):
         where = (t + 1 - 2 * way, h)
         return remote(
-            line_send.at[min(q, n_tok - 2)], line_recv.at[way, blocks[q]],
-            line_sem.at[way, min(q, n_tok - 2)], line_got.at[way, blocks[q]], where,
+            line_send.at[min(q, n_tok - 2), half_rows(i)],
+            line_recv.at[way, blocks[q], half_rows(i)],
+            line_sem.at[way, min(q, n_tok - 2), i], line_got.at[way, blocks[q], i], where,
         )
 
+    def send_half(q, way, i):
+        line_send[q, half_rows(i)] = kept_d[q, half_rows(i)].astype(BF16)
+        line_copy(q, way, i).start()
+
+    def add_half(q, way, i):
+        line_copy(q, way, i).wait_recv()
+        got = line_recv[way, blocks[q], half_rows(i)].astype(F32)
+        kept_d[q, half_rows(i)] = kept_d[q, half_rows(i)] + got
+
     def send_line(q, way):
-        line_send[q] = kept_d[q].astype(BF16)
-        line_copy(q, way).start()
+        for i in range(2):
+            send_half(q, way, i)
 
     def add_line(q, way):
-        line_copy(q, way).wait_recv()
-        kept_d[q] = kept_d[q] + line_recv[way, blocks[q]].astype(F32)
+        for i in range(2):
+            add_half(q, way, i)
+
+    def wait_line(q, way):
+        for i in range(2):
+            line_copy(q, way, i).wait_send()
 
     def start_line(q):
         pl.when((blocks[q] > t) & (t == 0))(lambda: send_line(q, 0))
@@ -480,8 +497,9 @@
 
     def over_line(q):
         def add_and_send(way):
-            add_line(q, way)
-            send_line(q, way)
+            for i in range(2):
+                add_half(q, way, i)
+                send_half(q, way, i)
 
         pl.when((blocks[q] > t) & (t > 0))(lambda: add_and_send(0))
         pl.when((blocks[q] < t) & (t < n_tok - 1))(lambda: add_and_send(1))
@@ -555,8 +573,8 @@
         value = value + all_t[k].astype(F32)
     terms_out[...] = value
     for q in range(final):
-        pl.when(blocks[q] > t)(lambda: line_copy(q, 0).wait_send())
-        pl.when(blocks[q] < t)(lambda: line_copy(q, 1).wait_send())
+        pl.when(blocks[q] > t)(lambda: wait_line(q, 0))
+        pl.when(blocks[q] < t)(lambda: wait_line(q, 1))
     for j in range(n_tok):
         act_along(j, wait_send)
         for p in range(n_part):
@@ -643,8 +661,8 @@
             sems((2, n_tok + 1, n_chip)),
             sems((2, n_tok + 1, 2)),
             sems((2, n_tok + 1, 2)),
-            sems((2, n_tok - 1)),
-            sems((2, n_tok)),
+            sems((2, n_tok - 1, 2)),
+            sems((2, n_tok, 2)),
             sems((2, n_tok - 1)),
             sems((2, n_tok, n_part, 2)),
             sems((n_tok, n_part, 2)),

time: 104 us -> 104 us (level)
  no operation moved by 1% of the time
where the time goes in v8:
time: 104 us
  Pallas kernels  103 us (99%)
    pallas_call x1, Pallas kernels, fused(): pl.pallas_call(functools.partial(fused_kernel, n_tok, n_hid, n_part, scal...  101 us

profile of v8, /device:TPU:0, one launch (start us, length us, event | category | flops | bytes accessed | tf_op | source)
XLA Modules:
  0.0 103.6 jit_solution(11476601851272544889)
XLA Ops:
  0.6 101.4 %shard_map.119 = (f32[512,128]{1,0:T(8,128)S(1)}, f32[256,128]{1,0:T(8,128)S(1)}, bf16[2048,128]{1,0:T(8,128)(2,1)S(1)}, bf16[128,2048]{1,0:T(8,128)(2,1)S(1)}) custom-call(bf16[512,128]{1,0:T(8,128)(2,1)} %tokens.1, bf16[512,128]{1,0:T(8,128)(2,1)} %cotangent.1, bf16[256,2048]{1,0:T(8,128)(2,1)} %w_in.1, bf16[2048,256]{1,0:T(8,128)(2,1)} %w_out.1, ...), custom_call_target="tpu_custom_call" | custom-call | tf_op jit(solution)/shard_map/pallas_call | solution.py:602
  102.1 1.5 %shard_map.120 = (f32[512,128]{1,0:T(8,128)}, f32[128,128]{1,0:T(8,128)}, f32[128,2048]{1,0:T(8,128)}, f32[2048,128]{1,0:T(8,128)}, f32[128,128]{1,0:T(8,128)}) custom-call(f32[512,128]{1,0:T(8,128)S(1)} %get-tuple-element.9.dx, f32[256,128]{1,0:T(8,128)S(1)} %get-tuple-element.10.terms, bf16[2048,128]{1,0:T(8,128)(2,1)S(1)} %get-tuple-element.11.oa, ...), custom_call_target="tpu_custom_call" | custom-call | tf_op jit(solution)/shard_map/pallas_call | solution.py:693
